TPU v7x, 32 devices: a whole 2x2x4 slice. The times are simulated.
32 devices in a mesh: feat: 8 (over z, core), col: 4 (over y, x).
Axes of the slice: x: 2, y: 2, z: 4, core: 2. Of those that a mesh axis runs over, the one named last changes fastest.
Arguments:
- self_feats: bfloat16 [4096, 128], P(('feat', 'col')), may hold values from -6 to 6
- neighbour_feats: bfloat16 [128, 16384], P('feat', 'col'), may hold values from -6 to 6
- tiles: bfloat16 [1024, 128, 128], P('col'), may hold values from 0 to 1, as said below
- tile_rows: int32 [1024], P('col'), may hold values from 0 to 31, as said below
- tile_cols: int32 [1024], P('col'), may hold values from 0 to 31
- tile_count: int32 [4], P('col'), may hold values from 1 to 256, 768 in all
- owner_order: int32 [32], replicated, may hold values from 0 to 31, as said below
- degree: int32 [4096], P(('feat', 'col')), may hold values from 64 to 192
- w_self: bfloat16 [128, 256], replicated, may hold values from -0.5 to 0.5
- w_neigh: bfloat16 [128, 256], replicated, may hold values from -0.5 to 0.5
- bias: float32 [256], replicated, may hold values from -3 to 3
- upstream: bfloat16 [4096, 256], P(('feat', 'col')), may hold values from -6 to 6
Outputs:
- hidden_out: bfloat16 [4096, 256], P(('feat', 'col'))
- neigh_grad: bfloat16 [128, 16384], P('feat', 'col')
Inputs may be any that keep to these rules, and one draw needn't show every extreme that they name: `tiles`: every entry is 0 or 1. `tile_count`: slots at or after a group's count are ignored; some group has all 256 slots live. `owner_order`: a permutation of the row blocks. `tile_rows`: in every column group, slot s has a row block whose owner position p satisfies (p) % 4 == s % 4.
All inputs are finite; a program needn't handle non-finite values.
Results may differ from a plain program's by a relative error of at most 0.0065.
Values may be sent and summed in bfloat16 or wider, within the bound.
No kernel may reach another device: no remote copies, remote signals or barrier semaphores. Data moves between devices by JAX's collectives and lax.ppermute only.
A program may use at most 64 MiB of HBM per device.

v0:
```python
import jax
import jax.numpy as jnp
from jax import lax
from jax.experimental import pallas as pl
from jax.experimental.pallas import tpu as pltpu
from jax.sharding import PartitionSpec as P

CHUNK = 64
STACK = 8


def invert_order(order_ref, places):
    def body(position, carry):
        places[order_ref[position]] = position
        return carry

    lax.fori_loop(0, order_ref.shape[0], body, 0, unroll=8)


def tile_copy(tiles_hbm, tiles_vmem, sems, chunk):
    window = pl.ds(chunk * CHUNK, CHUNK)
    return pltpu.make_async_copy(tiles_hbm.at[window], tiles_vmem.at[window], sems.at[chunk])


def forward_kernel(
    rows_ref,
    cols_ref,
    count_ref,
    order_ref,
    feats_ref,
    tiles_hbm,
    partial_ref,
    tiles_ref,
    places,
    acc,
    sems,
):
    slots, tile_size, _ = tiles_ref.shape
    blocks_total, slice_width, _ = partial_ref.shape
    for chunk in range(slots // CHUNK):
        tile_copy(tiles_hbm, tiles_ref, sems, chunk).start()
    invert_order(order_ref, places)
    acc[...] = jnp.zeros_like(acc)
    count = count_ref[0]

    for first in range(0, slots, STACK):
        if first % CHUNK == 0:
            tile_copy(tiles_hbm, tiles_ref, sems, first // CHUNK).wait()
        group = range(first, first + STACK)
        starts = [pl.multiple_of(cols_ref[slot] * tile_size, tile_size) for slot in group]
        stacked = jnp.concatenate(
            [feats_ref[:, pl.ds(start, tile_size)] for start in starts], axis=0
        )
        crossed = lax.dot_general(
            stacked,
            tiles_ref[pl.ds(first, STACK)].reshape(STACK * tile_size, tile_size),
            (((1,), (1,)), ((), ())),
            preferred_element_type=jnp.float32,
        )
        for i, slot in enumerate(group):
            target = jnp.where(slot < count, places[rows_ref[slot]], blocks_total)
            acc[target] += crossed[
                i * slice_width : (i + 1) * slice_width, i * tile_size : (i + 1) * tile_size
            ]

    partial_ref[...] = acc[:blocks_total].astype(partial_ref.dtype)


def dense_kernel(
    got_ref,
    self_ref,
    degree_ref,
    w_self_ref,
    w_neigh_ref,
    bias_ref,
    upstream_ref,
    hidden_ref,
    back_ref,
    summed,
):
    nfeat, ncol, slice_width, tile_size = got_ref.shape
    for f in range(nfeat):
        summed[pl.ds(f * slice_width, slice_width), :] = jnp.sum(
            got_ref[f].astype(jnp.float32), axis=0
        )
    scale = lax.rsqrt(degree_ref[...].astype(jnp.float32))
    aggregate = (summed[...] * scale).astype(jnp.bfloat16)
    pre = jnp.dot(self_ref[...], w_self_ref[...], preferred_element_type=jnp.float32)
    pre = pre + lax.dot_general(
        aggregate, w_neigh_ref[...], (((0,), (0,)), ((), ())), preferred_element_type=jnp.float32
    )
    pre = pre + bias_ref[...]
    gate = jax.nn.sigmoid(pre)
    hidden_ref[...] = (pre * gate).astype(jnp.bfloat16)
    slope = gate * (1.0 + pre * (1.0 - gate))
    dpre = (upstream_ref[...].astype(jnp.float32) * slope).astype(jnp.bfloat16)
    dagg = lax.dot_general(
        w_neigh_ref[...], dpre, (((1,), (1,)), ((), ())), preferred_element_type=jnp.float32
    )
    back = dagg * scale
    for f in range(nfeat):
        piece = back[f * slice_width : (f + 1) * slice_width].astype(jnp.bfloat16)
        for c in range(ncol):
            back_ref[f, c] = piece


def backward_kernel(
    rows_ref,
    cols_ref,
    count_ref,
    order_ref,
    grads_ref,
    tiles_ref,
    out_ref,
    places,
    acc_even,
    acc_odd,
):
    slots, tile_size, _ = tiles_ref.shape
    slice_width = out_ref.shape[0]
    invert_order(order_ref, places)
    accs = (acc_even, acc_odd)
    for acc in accs:
        acc[...] = jnp.zeros_like(acc)
    col_blocks = out_ref.shape[1] // tile_size
    count = count_ref[0]
    blank = jnp.zeros((slice_width, tile_size), grads_ref.dtype)

    for first in range(0, slots, 2):
        even = grads_ref[places[rows_ref[first]]]
        odd = grads_ref[places[rows_ref[first + 1]]]
        diagonal = jnp.concatenate(
            [
                jnp.concatenate([even, blank], axis=1),
                jnp.concatenate([blank, odd], axis=1),
            ],
            axis=0,
        )
        pieces = jnp.dot(
            diagonal,
            tiles_ref[pl.ds(first, 2)].reshape(2 * tile_size, tile_size),
            preferred_element_type=jnp.float32,
        )
        for i, acc in enumerate(accs):
            target = jnp.where(first + i < count, cols_ref[first + i], col_blocks)
            acc[target] += pieces[i * slice_width : (i + 1) * slice_width]

    for block in range(col_blocks):
        total = acc_even[block] + acc_odd[block]
        out_ref[:, block * tile_size : (block + 1) * tile_size] = total.astype(out_ref.dtype)


VMEM = pl.BlockSpec(memory_space=pltpu.VMEM)
SMEM = pl.BlockSpec(memory_space=pltpu.SMEM)
ANY = pl.BlockSpec(memory_space=pl.ANY)


def local(
    self_feats,
    neighbour_feats,
    tiles,
    tile_rows,
    tile_cols,
    tile_count,
    owner_order,
    degree,
    w_self,
    w_neigh,
    bias,
    upstream,
):
    nfeat = lax.axis_size("feat")
    ncol = lax.axis_size("col")
    slots, tile_size, _ = tiles.shape
    slice_width, width = neighbour_feats.shape
    col_blocks = width // tile_size
    rows = self_feats.shape[0]
    blocks_total = owner_order.shape[0]
    assert rows == tile_size and blocks_total == nfeat * ncol
    params = pltpu.CompilerParams(vmem_limit_bytes=32 << 20)

    partial_value, tiles_kept = pl.pallas_call(
        forward_kernel,
        out_shape=(
            jax.ShapeDtypeStruct((blocks_total, slice_width, tile_size), jnp.bfloat16),
            pltpu.VMEM(tiles.shape, tiles.dtype),
        ),
        in_specs=[SMEM, SMEM, SMEM, SMEM, VMEM, ANY],
        out_specs=(VMEM, VMEM),
        scratch_shapes=[
            pltpu.SMEM((blocks_total,), jnp.int32),
            pltpu.VMEM((blocks_total + 1, slice_width, tile_size), jnp.float32),
            pltpu.SemaphoreType.DMA((slots // CHUNK,)),
        ],
        compiler_params=params,
        name="forward",
    )(tile_rows, tile_cols, tile_count, owner_order, neighbour_feats, tiles)

    got = lax.all_to_all(partial_value, ("feat", "col"), split_axis=0, concat_axis=0, tiled=True)

    hidden_out, back = pl.pallas_call(
        dense_kernel,
        out_shape=(
            jax.ShapeDtypeStruct(upstream.shape, jnp.bfloat16),
            jax.ShapeDtypeStruct((nfeat, ncol, slice_width, tile_size), jnp.bfloat16),
        ),
        in_specs=[VMEM] * 7,
        out_specs=(VMEM, VMEM),
        scratch_shapes=[pltpu.VMEM((nfeat * slice_width, tile_size), jnp.float32)],
        compiler_params=params,
        name="dense",
    )(
        got.reshape(nfeat, ncol, slice_width, tile_size),
        self_feats,
        degree.reshape(1, rows),
        w_self,
        w_neigh,
        bias.reshape(1, -1),
        upstream,
    )

    row_grads = lax.all_to_all(
        back.reshape(blocks_total, slice_width, tile_size),
        ("feat", "col"),
        split_axis=0,
        concat_axis=0,
        tiled=True,
    )

    neigh_grad = pl.pallas_call(
        backward_kernel,
        out_shape=jax.ShapeDtypeStruct(neighbour_feats.shape, jnp.bfloat16),
        in_specs=[SMEM, SMEM, SMEM, SMEM, VMEM, VMEM],
        out_specs=VMEM,
        scratch_shapes=[
            pltpu.SMEM((blocks_total,), jnp.int32),
            pltpu.VMEM((col_blocks + 1, slice_width, tile_size), jnp.float32),
            pltpu.VMEM((col_blocks + 1, slice_width, tile_size), jnp.float32),
        ],
        compiler_params=params,
        name="backward",
    )(
        tile_rows,
        tile_cols,
        tile_count,
        owner_order,
        row_grads,
        pltpu.with_memory_space_constraint(tiles_kept, pltpu.VMEM),
    )
    return (hidden_out, neigh_grad)


def solution(mesh):
    in_specs = (
        P(("feat", "col"), None),
        P("feat", "col"),
        P("col", None, None),
        P("col"),
        P("col"),
        P("col"),
        P(),
        P(("feat", "col")),
        P(),
        P(),
        P(),
        P(("feat", "col"), None),
    )
    out_specs = (P(("feat", "col"), None), P("feat", "col"))
    return jax.shard_map(local, mesh=mesh, in_specs=in_specs, out_specs=out_specs, check_vma=False)
```

profile of v0, /device:TPU:0, one launch (start us, length us, event | category | flops | bytes accessed | tf_op | source)
XLA Modules:
  0.0 41.2 jit_solution(6280624749730630639)
XLA Ops:
  0.6 0.0 copy-start.11
  0.6 0.0 copy-start.7
  1.3 0.0 copy-start
  1.3 3.4 %copy-done = bf16[256,128,128]{2,1,0:T(8,128)(2,1)S(1)} copy-done((bf16[256,128,128]{2,1,0:T(8,128)(2,1)S(1)}, bf16[256,128,128]{2,1,0:T(8,128)(2,1)}, u32[]{:S(2)}) %copy-start) | copy-done | bytes 8388632
  4.7 0.9 %copy-done.1 = bf16[16,4096]{1,0:T(8,128)(2,1)S(1)} copy-done((bf16[16,4096]{1,0:T(8,128)(2,1)S(1)}, bf16[16,4096]{1,0:T(8,128)(2,1)}, u32[]{:S(2)}) %copy-start.1) | copy-done | bytes 131096
  5.6 0.7 %copy-done.6 = s32[256]{0:T(256)S(1)} copy-done((s32[256]{0:T(256)S(1)}, s32[256]{0:T(256)}, u32[]{:S(2)}) %copy-start.6) | copy-done | bytes 1048
  6.3 0.7 %copy-done.8 = s32[256]{0:T(256)S(1)} copy-done((s32[256]{0:T(256)S(1)}, s32[256]{0:T(256)}, u32[]{:S(2)}) %copy-start.8) | copy-done | bytes 1048
  7.0 0.7 %copy-done.10 = s32[32]{0:T(128)S(1)} copy-done((s32[32]{0:T(128)S(1)}, s32[32]{0:T(128)}, u32[]{:S(2)}) %copy-start.10) | copy-done | bytes 152
  7.6 0.0 copy-start.12
  7.6 0.0 copy-start.13
  7.7 0.0 copy-start.9
  7.7 4.2 %forward.1 = (bf16[32,16,128]{2,1,0:T(8,128)(2,1)S(1)}, bf16[256,128,128]{2,1,0:T(8,128)(2,1)S(1)}) custom-call(s32[256]{0:T(256)S(1)} %copy-done.6, s32[256]{0:T(256)S(1)} %copy-done.8, s32[1]{0:T(128)S(6)} %copy.14.count_ref, s32[32]{0:T(128)S(1)} %copy-done.10, bf16[16,4096]{1,0:T(8,128)(2,1)S(1)} %copy-done.1, bf16[256,128,128]{2,1,0:T(8,128)(2,1)S(1)} %copy-done), custom_call_target="tpu_custom_call" | custom-call | tf_op jit(solution)/shard_map/forward/pallas_call | solution.py:182
  11.9 15.6 %all_to_all.10 = bf16[32,16,128]{2,1,0:T(8,128)(2,1)S(1)} all-to-all(bf16[32,16,128]{2,1,0:T(8,128)(2,1)S(1)} %get-tuple-element.6), channel_id=1, replica_groups=mesh['feat'=8,'col'=4] {'feat','col'}, dimensions={0} | all-to-all | bytes 262144 | tf_op jit(solution)/shard_map/all_to_all | solution.py:199
  27.5 0.0 copy-done.2
  27.5 0.0 copy-done.3
  27.5 0.0 copy-done.4
  27.5 0.0 copy-done.5
  27.5 0.0 copy-done.12
  27.5 0.0 copy-done.13
  27.5 0.9 %dense.1 = (bf16[128,256]{1,0:T(8,128)(2,1)}, bf16[8,4,16,128]{3,2,1,0:T(8,128)(2,1)S(1)}) custom-call(bf16[8,4,16,128]{3,2,1,0:T(8,128)(2,1)S(1)} %bitcast.4, bf16[128,128]{1,0:T(8,128)(2,1)S(1)} %copy-done.5, s32[1,128]{1,0:T(1,128)S(1)} %bitcast.7, bf16[128,256]{1,0:T(8,128)(2,1)S(1)} %copy-done.2, bf16[128,256]{1,0:T(8,128)(2,1)S(1)} %copy-done.3, ...), custom_call_target="tpu_custom_call" | custom-call | tf_op jit(solution)/shard_map/dense/pallas_call | solution.py:201
  28.4 10.1 %all_to_all.11.grads_ref = bf16[32,16,128]{2,1,0:T(8,128)(2,1)S(1)} all-to-all(bf16[32,16,128]{2,1,0:T(8,128)(2,1)S(1)} %bitcast.5), channel_id=1, replica_groups=mesh['feat'=8,'col'=4] {'feat','col'}, dimensions={0} | all-to-all | bytes 262144 | tf_op jit(solution)/shard_map/all_to_all | solution.py:222
  38.5 0.0 copy-done.11
  38.5 0.0 copy-done.7
  38.5 2.7 %backward.1 = bf16[16,4096]{1,0:T(8,128)(2,1)} custom-call(s32[256]{0:T(256)S(1)} %copy-done.7, s32[256]{0:T(256)S(1)} %copy-done.9, s32[1]{0:T(128)S(6)} %copy.14.count_ref, s32[32]{0:T(128)S(1)} %copy-done.11, bf16[32,16,128]{2,1,0:T(8,128)(2,1)S(1)} %all_to_all.11.grads_ref, bf16[256,128,128]{2,1,0:T(8,128)(2,1)S(1)} %get-tuple-element.9.tiles_ref), custom_call_target="tpu_custom_call" | custom-call | tf_op jit(solution)/shard_map/backward/pallas_call | solution.py:230
  (9 shorter events, 0.0 us)
Async XLA Ops:
  0.6 37.9 %copy-start.11 = (s32[32]{0:T(128)S(1)}, s32[32]{0:T(128)}, u32[]{:S(2)}) copy-start(s32[32]{0:T(128)} %order_ref.3) | copy-start | bytes 388
  0.6 37.8 %copy-start.7 = (s32[256]{0:T(256)S(1)}, s32[256]{0:T(256)}, u32[]{:S(2)}) copy-start(s32[256]{0:T(256)} %rows_ref.3) | copy-start | bytes 3076
  1.3 3.4 %copy-start = (bf16[256,128,128]{2,1,0:T(8,128)(2,1)S(1)}, bf16[256,128,128]{2,1,0:T(8,128)(2,1)}, u32[]{:S(2)}) copy-start(bf16[256,128,128]{2,1,0:T(8,128)(2,1)} %tiles_hbm.1) | copy-start | bytes 25165828
  4.7 0.9 %copy-start.1 = (bf16[16,4096]{1,0:T(8,128)(2,1)S(1)}, bf16[16,4096]{1,0:T(8,128)(2,1)}, u32[]{:S(2)}) copy-start(bf16[16,4096]{1,0:T(8,128)(2,1)} %feats_ref.1) | copy-start | bytes 393220
  5.6 0.7 %copy-start.6 = (s32[256]{0:T(256)S(1)}, s32[256]{0:T(256)}, u32[]{:S(2)}) copy-start(s32[256]{0:T(256)} %rows_ref.3) | copy-start | bytes 3076
  6.3 0.7 %copy-start.8 = (s32[256]{0:T(256)S(1)}, s32[256]{0:T(256)}, u32[]{:S(2)}) copy-start(s32[256]{0:T(256)} %cols_ref.3) | copy-start | bytes 3076
  7.0 0.7 %copy-start.10 = (s32[32]{0:T(128)S(1)}, s32[32]{0:T(128)}, u32[]{:S(2)}) copy-start(s32[32]{0:T(128)} %order_ref.3) | copy-start | bytes 388
  7.6 19.8 %copy-start.2 = (bf16[128,256]{1,0:T(8,128)(2,1)S(1)}, bf16[128,256]{1,0:T(8,128)(2,1)}, u32[]{:S(2)}) copy-start(bf16[128,256]{1,0:T(8,128)(2,1)} %w_self_ref.1) | copy-start | bytes 196612
  7.6 19.8 %copy-start.3 = (bf16[128,256]{1,0:T(8,128)(2,1)S(1)}, bf16[128,256]{1,0:T(8,128)(2,1)}, u32[]{:S(2)}) copy-start(bf16[128,256]{1,0:T(8,128)(2,1)} %w_neigh_ref.1) | copy-start | bytes 196612
  7.6 19.8 %copy-start.4 = (bf16[128,256]{1,0:T(8,128)(2,1)S(1)}, bf16[128,256]{1,0:T(8,128)(2,1)}, u32[]{:S(2)}) copy-start(bf16[128,256]{1,0:T(8,128)(2,1)} %upstream_ref.1) | copy-start | bytes 196612
  7.6 19.8 %copy-start.5 = (bf16[128,128]{1,0:T(8,128)(2,1)S(1)}, bf16[128,128]{1,0:T(8,128)(2,1)}, u32[]{:S(2)}) copy-start(bf16[128,128]{1,0:T(8,128)(2,1)} %self_ref.1) | copy-start | bytes 98308
  7.6 19.8 %copy-start.12 = (f32[256]{0:T(256)S(1)}, f32[256]{0:T(256)}, u32[]{:S(2)}) copy-start(f32[256]{0:T(256)} %param.22) | copy-start | bytes 3076
  7.6 19.8 %copy-start.13 = (s32[128]{0:T(128)S(1)}, s32[128]{0:T(128)}, u32[]{:S(2)}) copy-start(s32[128]{0:T(128)} %param.19) | copy-start | bytes 1540
  7.7 30.8 %copy-start.9 = (s32[256]{0:T(256)S(1)}, s32[256]{0:T(256)}, u32[]{:S(2)}) copy-start(s32[256]{0:T(256)} %cols_ref.3) | copy-start | bytes 3076
where the time goes:
time: 41.5 us; the launch traced here: 41.2 us
  blocking collectives  25.7 us (62%)
  Pallas kernels  7.81 us (19%)
  local copies, waits for them, and re-layouts  6.33 us (15%)
  between operations  1.4 us (3%)
    all_to_all x1, blocking collectives, local(): lax.all_to_all(partial_value, ('feat', 'col'), split_axis=0, concat_axis=...  15.6 us
    all_to_all x1, blocking collectives, local(): lax.all_to_all(back.reshape(blocks_total, slice_width, tile_size), ('feat...  10.1 us
    unnamed x28, local copies, waits for them, and re-layouts  6.33 us
    pallas_call x1, Pallas kernels, local(): pl.pallas_call(forward_kernel, out_shape=(jax.ShapeDtypeStruct((blocks_to...  4.21 us
    pallas_call x1, Pallas kernels, local(): pl.pallas_call(backward_kernel, out_shape=jax.ShapeDtypeStruct(neighbour_...  2.69 us
    pallas_call x1, Pallas kernels, local(): pl.pallas_call(dense_kernel, out_shape=(jax.ShapeDtypeStruct(upstream.sha...  0.9 us

commit v1 on v0

--- a/solution.py
+++ b/solution.py
@@ -17,30 +17,58 @@
     lax.fori_loop(0, order_ref.shape[0], body, 0, unroll=8)
 
 
+def fetch(pairs, sems):
+    copies = [
+        pltpu.make_async_copy(source, target, sems.at[i])
+        for i, (source, target) in enumerate(pairs)
+    ]
+    for copy in copies:
+        copy.start()
+    return copies
+
+
 def tile_copy(tiles_hbm, tiles_vmem, sems, chunk):
     window = pl.ds(chunk * CHUNK, CHUNK)
     return pltpu.make_async_copy(tiles_hbm.at[window], tiles_vmem.at[window], sems.at[chunk])
 
 
 def forward_kernel(
+    order_hbm,
+    rows_hbm,
+    cols_hbm,
+    count_hbm,
+    feats_hbm,
+    tiles_hbm,
+    partial_ref,
+    tiles_ref,
+    order_ref,
     rows_ref,
     cols_ref,
     count_ref,
-    order_ref,
     feats_ref,
-    tiles_hbm,
-    partial_ref,
-    tiles_ref,
     places,
     acc,
+    small_sems,
     sems,
 ):
     slots, tile_size, _ = tiles_ref.shape
     blocks_total, slice_width, _ = partial_ref.shape
+    small = fetch(
+        [
+            (order_hbm, order_ref),
+            (rows_hbm, rows_ref),
+            (cols_hbm, cols_ref),
+            (count_hbm, count_ref),
+            (feats_hbm, feats_ref),
+        ],
+        small_sems,
+    )
     for chunk in range(slots // CHUNK):
         tile_copy(tiles_hbm, tiles_ref, sems, chunk).start()
+    acc[...] = jnp.zeros_like(acc)
+    for copy in small:
+        copy.wait()
     invert_order(order_ref, places)
-    acc[...] = jnp.zeros_like(acc)
     count = count_ref[0]
 
     for first in range(0, slots, STACK):
@@ -105,23 +133,39 @@
 
 
 def backward_kernel(
+    order_hbm,
+    rows_hbm,
+    cols_hbm,
+    count_hbm,
+    grads_ref,
+    tiles_ref,
+    out_ref,
+    order_ref,
     rows_ref,
     cols_ref,
     count_ref,
-    order_ref,
-    grads_ref,
-    tiles_ref,
-    out_ref,
     places,
     acc_even,
     acc_odd,
+    small_sems,
 ):
     slots, tile_size, _ = tiles_ref.shape
     slice_width = out_ref.shape[0]
-    invert_order(order_ref, places)
+    small = fetch(
+        [
+            (order_hbm, order_ref),
+            (rows_hbm, rows_ref),
+            (cols_hbm, cols_ref),
+            (count_hbm, count_ref),
+        ],
+        small_sems,
+    )
     accs = (acc_even, acc_odd)
     for acc in accs:
         acc[...] = jnp.zeros_like(acc)
+    for copy in small:
+        copy.wait()
+    invert_order(order_ref, places)
     col_blocks = out_ref.shape[1] // tile_size
     count = count_ref[0]
     blank = jnp.zeros((slice_width, tile_size), grads_ref.dtype)
@@ -151,8 +195,11 @@
 
 
 VMEM = pl.BlockSpec(memory_space=pltpu.VMEM)
-SMEM = pl.BlockSpec(memory_space=pltpu.SMEM)
 ANY = pl.BlockSpec(memory_space=pl.ANY)
+
+
+def in_hbm(x):
+    return pltpu.with_memory_space_constraint(x, pltpu.HBM)
 
 
 def local(
@@ -177,6 +224,8 @@
     rows = self_feats.shape[0]
     blocks_total = owner_order.shape[0]
     assert rows == tile_size and blocks_total == nfeat * ncol
+    index_arrays = [in_hbm(x) for x in (owner_order, tile_rows, tile_cols)] + [tile_count]
+    index_scratch = [pltpu.SMEM(x.shape, x.dtype) for x in index_arrays]
     params = pltpu.CompilerParams(vmem_limit_bytes=32 << 20)
 
     partial_value, tiles_kept = pl.pallas_call(
@@ -185,16 +234,19 @@
             jax.ShapeDtypeStruct((blocks_total, slice_width, tile_size), jnp.bfloat16),
             pltpu.VMEM(tiles.shape, tiles.dtype),
         ),
-        in_specs=[SMEM, SMEM, SMEM, SMEM, VMEM, ANY],
+        in_specs=[ANY] * 6,
         out_specs=(VMEM, VMEM),
-        scratch_shapes=[
+        scratch_shapes=index_scratch
+        + [
+            pltpu.VMEM(neighbour_feats.shape, neighbour_feats.dtype),
             pltpu.SMEM((blocks_total,), jnp.int32),
             pltpu.VMEM((blocks_total + 1, slice_width, tile_size), jnp.float32),
+            pltpu.SemaphoreType.DMA((5,)),
             pltpu.SemaphoreType.DMA((slots // CHUNK,)),
         ],
         compiler_params=params,
         name="forward",
-    )(tile_rows, tile_cols, tile_count, owner_order, neighbour_feats, tiles)
+    )(*index_arrays, in_hbm(neighbour_feats), in_hbm(tiles))
 
     got = lax.all_to_all(partial_value, ("feat", "col"), split_axis=0, concat_axis=0, tiled=True)
 
@@ -230,20 +282,19 @@
     neigh_grad = pl.pallas_call(
         backward_kernel,
         out_shape=jax.ShapeDtypeStruct(neighbour_feats.shape, jnp.bfloat16),
-        in_specs=[SMEM, SMEM, SMEM, SMEM, VMEM, VMEM],
+        in_specs=[ANY] * 4 + [VMEM] * 2,
         out_specs=VMEM,
-        scratch_shapes=[
+        scratch_shapes=index_scratch
+        + [
             pltpu.SMEM((blocks_total,), jnp.int32),
             pltpu.VMEM((col_blocks + 1, slice_width, tile_size), jnp.float32),
             pltpu.VMEM((col_blocks + 1, slice_width, tile_size), jnp.float32),
+            pltpu.SemaphoreType.DMA((4,)),
         ],
         compiler_params=params,
         name="backward",
     )(
-        tile_rows,
-        tile_cols,
-        tile_count,
-        owner_order,
+        *index_arrays,
         row_grads,
         pltpu.with_memory_space_constraint(tiles_kept, pltpu.VMEM),
     )

time: 41.5 us -> 37.6 us (0.906)
  local copies, waits for them, and re-layouts: 6.33 us -> 0.03 us
  Pallas kernels: 7.81 us -> 10.3 us
    unnamed x28 -> x12, local copies, waits for them, and re-layouts: 6.33 us -> 0.03 us
    pallas_call x1, Pallas kernels: 4.21 us -> 6.42 us  [local(): pl.pallas_call(forward_kernel, out_shape=(jax.ShapeDtypeStruct((blocks_to...]
where the time goes in v1:
time: 37.6 us; the launch traced here: 37.3 us
  blocking collectives  25.6 us (68%)
  Pallas kernels  10.3 us (27%)
  between operations  1.44 us (4%)
    all_to_all x1, blocking collectives, local(): lax.all_to_all(partial_value, ('feat', 'col'), split_axis=0, concat_axis=...  15.5 us
    all_to_all x1, blocking collectives, local(): lax.all_to_all(back.reshape(blocks_total, slice_width, tile_size), ('feat...  10.1 us
    pallas_call x1, Pallas kernels, local(): pl.pallas_call(forward_kernel, out_shape=(jax.ShapeDtypeStruct((blocks_to...  6.42 us
    pallas_call x1, Pallas kernels, local(): pl.pallas_call(backward_kernel, out_shape=jax.ShapeDtypeStruct(neighbour_...  2.93 us
    pallas_call x1, Pallas kernels, local(): pl.pallas_call(dense_kernel, out_shape=(jax.ShapeDtypeStruct(upstream.sha...  0.9 us

profile of v1, /device:TPU:0, one launch (start us, length us, event | category | flops | bytes accessed | tf_op | source)
XLA Modules:
  0.0 37.3 jit_solution(13572211155238561260)
XLA Ops:
  0.6 0.0 copy-start.2
  0.6 0.0 copy-start.4
  0.7 0.0 copy-start.1
  0.7 0.0 copy-start
  0.7 0.0 copy-start.5
  0.7 0.0 copy-start.3
  1.4 6.4 %forward.1 = (bf16[32,16,128]{2,1,0:T(8,128)(2,1)S(1)}, bf16[256,128,128]{2,1,0:T(8,128)(2,1)S(1)}) custom-call(s32[32]{0:T(128)} %order_hbm.3, s32[256]{0:T(256)} %rows_hbm.3, s32[256]{0:T(256)} %cols_hbm.3, s32[1]{0:T(128)S(6)} %copy.14.count_hbm, bf16[16,4096]{1,0:T(8,128)(2,1)} %feats_hbm.1, bf16[256,128,128]{2,1,0:T(8,128)(2,1)} %tiles_hbm.1), custom_call_target="tpu_custom_call" | custom-call | tf_op jit(solution)/shard_map/forward/pallas_call | solution.py:231
  7.8 15.5 %all_to_all.10 = bf16[32,16,128]{2,1,0:T(8,128)(2,1)S(1)} all-to-all(bf16[32,16,128]{2,1,0:T(8,128)(2,1)S(1)} %get-tuple-element.6), channel_id=1, replica_groups=mesh['feat'=8,'col'=4] {'feat','col'}, dimensions={0} | all-to-all | bytes 262144 | tf_op jit(solution)/shard_map/all_to_all | solution.py:251
  23.3 0.0 copy-done.2
  23.3 0.0 copy-done.4
  23.3 0.0 copy-done.1
  23.3 0.0 copy-done
  23.3 0.0 copy-done.5
  23.3 0.0 copy-done.3
  23.4 0.9 %dense.1 = (bf16[128,256]{1,0:T(8,128)(2,1)}, bf16[8,4,16,128]{3,2,1,0:T(8,128)(2,1)S(1)}) custom-call(bf16[8,4,16,128]{3,2,1,0:T(8,128)(2,1)S(1)} %bitcast.4, bf16[128,128]{1,0:T(8,128)(2,1)S(1)} %copy-done.3, s32[1,128]{1,0:T(1,128)S(1)} %bitcast.7, bf16[128,256]{1,0:T(8,128)(2,1)S(1)} %copy-done, bf16[128,256]{1,0:T(8,128)(2,1)S(1)} %copy-done.1, ...), custom_call_target="tpu_custom_call" | custom-call | tf_op jit(solution)/shard_map/dense/pallas_call | solution.py:253
  24.3 10.1 %all_to_all.11.grads_ref = bf16[32,16,128]{2,1,0:T(8,128)(2,1)S(1)} all-to-all(bf16[32,16,128]{2,1,0:T(8,128)(2,1)S(1)} %bitcast.5), channel_id=1, replica_groups=mesh['feat'=8,'col'=4] {'feat','col'}, dimensions={0} | all-to-all | bytes 262144 | tf_op jit(solution)/shard_map/all_to_all | solution.py:274
  34.3 2.9 %backward.1 = bf16[16,4096]{1,0:T(8,128)(2,1)} custom-call(s32[32]{0:T(128)} %order_hbm.3, s32[256]{0:T(256)} %rows_hbm.3, s32[256]{0:T(256)} %cols_hbm.3, s32[1]{0:T(128)S(6)} %copy.14.count_hbm, bf16[32,16,128]{2,1,0:T(8,128)(2,1)S(1)} %all_to_all.11.grads_ref, bf16[256,128,128]{2,1,0:T(8,128)(2,1)S(1)} %get-tuple-element.9.tiles_ref), custom_call_target="tpu_custom_call" | custom-call | tf_op jit(solution)/shard_map/backward/pallas_call | solution.py:282
Async XLA Ops:
  0.6 22.7 %copy-start.2 = (bf16[128,256]{1,0:T(8,128)(2,1)S(1)}, bf16[128,256]{1,0:T(8,128)(2,1)}, u32[]{:S(2)}) copy-start(bf16[128,256]{1,0:T(8,128)(2,1)} %upstream_ref.1) | copy-start | bytes 196612
  0.6 22.7 %copy-start.4 = (f32[256]{0:T(256)S(1)}, f32[256]{0:T(256)}, u32[]{:S(2)}) copy-start(f32[256]{0:T(256)} %param.22) | copy-start | bytes 3076
  0.7 22.7 %copy-start.1 = (bf16[128,256]{1,0:T(8,128)(2,1)S(1)}, bf16[128,256]{1,0:T(8,128)(2,1)}, u32[]{:S(2)}) copy-start(bf16[128,256]{1,0:T(8,128)(2,1)} %w_neigh_ref.1) | copy-start | bytes 196612
  0.7 22.7 %copy-start = (bf16[128,256]{1,0:T(8,128)(2,1)S(1)}, bf16[128,256]{1,0:T(8,128)(2,1)}, u32[]{:S(2)}) copy-start(bf16[128,256]{1,0:T(8,128)(2,1)} %w_self_ref.1) | copy-start | bytes 196612
  0.7 22.7 %copy-start.5 = (s32[128]{0:T(128)S(1)}, s32[128]{0:T(128)}, u32[]{:S(2)}) copy-start(s32[128]{0:T(128)} %param.19) | copy-start | bytes 1540
  0.7 22.7 %copy-start.3 = (bf16[128,128]{1,0:T(8,128)(2,1)S(1)}, bf16[128,128]{1,0:T(8,128)(2,1)}, u32[]{:S(2)}) copy-start(bf16[128,128]{1,0:T(8,128)(2,1)} %self_ref.1) | copy-start | bytes 98308

commit v2 on v1

--- a/solution.py
+++ b/solution.py
@@ -6,7 +6,6 @@
 from jax.sharding import PartitionSpec as P
 
 CHUNK = 64
-STACK = 8
 
 
 def invert_order(order_ref, places):
@@ -25,6 +24,13 @@
     for copy in copies:
         copy.start()
     return copies
+
+
+def block_diagonal(even, odd):
+    blank = jnp.zeros_like(even)
+    return jnp.concatenate(
+        [jnp.concatenate([even, blank], axis=1), jnp.concatenate([blank, odd], axis=1)], axis=0
+    )
 
 
 def tile_copy(tiles_hbm, tiles_vmem, sems, chunk):
@@ -47,12 +53,14 @@
     count_ref,
     feats_ref,
     places,
-    acc,
     small_sems,
     sems,
+    *accs,
 ):
     slots, tile_size, _ = tiles_ref.shape
     blocks_total, slice_width, _ = partial_ref.shape
+    ncol = len(accs)
+    spare = blocks_total // ncol
     small = fetch(
         [
             (order_hbm, order_ref),
@@ -65,33 +73,36 @@
     )
     for chunk in range(slots // CHUNK):
         tile_copy(tiles_hbm, tiles_ref, sems, chunk).start()
-    acc[...] = jnp.zeros_like(acc)
+    for acc in accs:
+        acc[...] = jnp.zeros_like(acc)
     for copy in small:
         copy.wait()
     invert_order(order_ref, places)
     count = count_ref[0]
-
-    for first in range(0, slots, STACK):
+    zero, one, two = (jnp.asarray(v, tiles_ref.dtype) for v in (0, 1, 2))
+
+    for first in range(0, slots, 2):
         if first % CHUNK == 0:
             tile_copy(tiles_hbm, tiles_ref, sems, first // CHUNK).wait()
-        group = range(first, first + STACK)
-        starts = [pl.multiple_of(cols_ref[slot] * tile_size, tile_size) for slot in group]
-        stacked = jnp.concatenate(
-            [feats_ref[:, pl.ds(start, tile_size)] for start in starts], axis=0
-        )
-        crossed = lax.dot_general(
-            stacked,
-            tiles_ref[pl.ds(first, STACK)].reshape(STACK * tile_size, tile_size),
-            (((1,), (1,)), ((), ())),
+        pair = (first, first + 1)
+        feats = [
+            feats_ref[:, pl.ds(pl.multiple_of(cols_ref[slot] * tile_size, tile_size), tile_size)]
+            for slot in pair
+        ]
+        packed = (tiles_ref[first] + two * tiles_ref[first + 1]).T
+        odd = jnp.where(packed >= two, one, zero)
+        even = packed - two * odd
+        pieces = jnp.dot(
+            block_diagonal(*feats),
+            jnp.concatenate([even, odd], axis=0),
             preferred_element_type=jnp.float32,
         )
-        for i, slot in enumerate(group):
-            target = jnp.where(slot < count, places[rows_ref[slot]], blocks_total)
-            acc[target] += crossed[
-                i * slice_width : (i + 1) * slice_width, i * tile_size : (i + 1) * tile_size
-            ]
-
-    partial_ref[...] = acc[:blocks_total].astype(partial_ref.dtype)
+        for i, slot in enumerate(pair):
+            target = jnp.where(slot < count, places[rows_ref[slot]] // ncol, spare)
+            accs[slot % ncol][target] += pieces[i * slice_width : (i + 1) * slice_width]
+
+    for block in range(blocks_total):
+        partial_ref[block] = accs[block % ncol][block // ncol].astype(partial_ref.dtype)
 
 
 def dense_kernel(
@@ -133,55 +144,31 @@
 
 
 def backward_kernel(
-    order_hbm,
-    rows_hbm,
-    cols_hbm,
-    count_hbm,
-    grads_ref,
-    tiles_ref,
-    out_ref,
     order_ref,
     rows_ref,
     cols_ref,
     count_ref,
+    grads_ref,
+    tiles_ref,
+    out_ref,
     places,
     acc_even,
     acc_odd,
-    small_sems,
 ):
     slots, tile_size, _ = tiles_ref.shape
     slice_width = out_ref.shape[0]
-    small = fetch(
-        [
-            (order_hbm, order_ref),
-            (rows_hbm, rows_ref),
-            (cols_hbm, cols_ref),
-            (count_hbm, count_ref),
-        ],
-        small_sems,
-    )
+    invert_order(order_ref, places)
     accs = (acc_even, acc_odd)
     for acc in accs:
         acc[...] = jnp.zeros_like(acc)
-    for copy in small:
-        copy.wait()
-    invert_order(order_ref, places)
     col_blocks = out_ref.shape[1] // tile_size
     count = count_ref[0]
-    blank = jnp.zeros((slice_width, tile_size), grads_ref.dtype)
 
     for first in range(0, slots, 2):
         even = grads_ref[places[rows_ref[first]]]
         odd = grads_ref[places[rows_ref[first + 1]]]
-        diagonal = jnp.concatenate(
-            [
-                jnp.concatenate([even, blank], axis=1),
-                jnp.concatenate([blank, odd], axis=1),
-            ],
-            axis=0,
-        )
         pieces = jnp.dot(
-            diagonal,
+            block_diagonal(even, odd),
             tiles_ref[pl.ds(first, 2)].reshape(2 * tile_size, tile_size),
             preferred_element_type=jnp.float32,
         )
@@ -195,6 +182,7 @@
 
 
 VMEM = pl.BlockSpec(memory_space=pltpu.VMEM)
+SMEM = pl.BlockSpec(memory_space=pltpu.SMEM)
 ANY = pl.BlockSpec(memory_space=pl.ANY)
 
 
@@ -240,10 +228,10 @@
         + [
             pltpu.VMEM(neighbour_feats.shape, neighbour_feats.dtype),
             pltpu.SMEM((blocks_total,), jnp.int32),
-            pltpu.VMEM((blocks_total + 1, slice_width, tile_size), jnp.float32),
             pltpu.SemaphoreType.DMA((5,)),
             pltpu.SemaphoreType.DMA((slots // CHUNK,)),
-        ],
+        ]
+        + [pltpu.VMEM((blocks_total // ncol + 1, slice_width, tile_size), jnp.float32)] * ncol,
         compiler_params=params,
         name="forward",
     )(*index_arrays, in_hbm(neighbour_feats), in_hbm(tiles))
@@ -282,19 +270,20 @@
     neigh_grad = pl.pallas_call(
         backward_kernel,
         out_shape=jax.ShapeDtypeStruct(neighbour_feats.shape, jnp.bfloat16),
-        in_specs=[ANY] * 4 + [VMEM] * 2,
+        in_specs=[SMEM] * 4 + [VMEM] * 2,
         out_specs=VMEM,
-        scratch_shapes=index_scratch
-        + [
+        scratch_shapes=[
             pltpu.SMEM((blocks_total,), jnp.int32),
             pltpu.VMEM((col_blocks + 1, slice_width, tile_size), jnp.float32),
             pltpu.VMEM((col_blocks + 1, slice_width, tile_size), jnp.float32),
-            pltpu.SemaphoreType.DMA((4,)),
         ],
         compiler_params=params,
         name="backward",
     )(
-        *index_arrays,
+        owner_order,
+        tile_rows,
+        tile_cols,
+        tile_count,
         row_grads,
         pltpu.with_memory_space_constraint(tiles_kept, pltpu.VMEM),
     )

time: 37.6 us -> 37.3 us (level)
  no operation moved by 1% of the time
where the time goes in v2:
time: 37.3 us; the launch traced here: 37.1 us
  blocking collectives  25.6 us (69%)
  Pallas kernels  10 us (27%)
  between operations  1.49 us (4%)
    all_to_all x1, blocking collectives, local(): lax.all_to_all(partial_value, ('feat', 'col'), split_axis=0, concat_axis=...  15.5 us
    all_to_all x1, blocking collectives, local(): lax.all_to_all(back.reshape(blocks_total, slice_width, tile_size), ('feat...  10.1 us
    pallas_call x1, Pallas kernels, local(): pl.pallas_call(forward_kernel, out_shape=(jax.ShapeDtypeStruct((blocks_to...  6.41 us
    pallas_call x1, Pallas kernels, local(): pl.pallas_call(backward_kernel, out_shape=jax.ShapeDtypeStruct(neighbour_...  2.69 us
    pallas_call x1, Pallas kernels, local(): pl.pallas_call(dense_kernel, out_shape=(jax.ShapeDtypeStruct(upstream.sha...  0.9 us

profile of v2, /device:TPU:0, one launch (start us, length us, event | category | flops | bytes accessed | tf_op | source)
XLA Modules:
  0.0 37.1 jit_solution(10269892577936161288)
XLA Ops:
  0.6 0.0 copy-start.6
  0.6 0.0 copy-start.5
  0.7 0.0 copy-start.4
  0.7 0.0 copy-start.2
  0.7 0.0 copy-start.7
  0.7 0.0 copy-start.1
  0.7 0.0 copy-start
  0.7 0.0 copy-start.8
  0.7 0.0 copy-start.3
  1.5 6.4 %forward.1 = (bf16[32,16,128]{2,1,0:T(8,128)(2,1)S(1)}, bf16[256,128,128]{2,1,0:T(8,128)(2,1)S(1)}) custom-call(s32[32]{0:T(128)} %order_ref.1, s32[256]{0:T(256)} %rows_ref.1, s32[256]{0:T(256)} %cols_ref.1, s32[1]{0:T(128)S(6)} %copy.14.count_hbm.count_ref, bf16[16,4096]{1,0:T(8,128)(2,1)} %feats_hbm.1, bf16[256,128,128]{2,1,0:T(8,128)(2,1)} %tiles_hbm.1), custom_call_target="tpu_custom_call" | custom-call | tf_op jit(solution)/shard_map/forward/pallas_call | solution.py:219
  7.9 15.5 %all_to_all.10 = bf16[32,16,128]{2,1,0:T(8,128)(2,1)S(1)} all-to-all(bf16[32,16,128]{2,1,0:T(8,128)(2,1)S(1)} %get-tuple-element.6), channel_id=1, replica_groups=mesh['feat'=8,'col'=4] {'feat','col'}, dimensions={0} | all-to-all | bytes 262144 | tf_op jit(solution)/shard_map/all_to_all | solution.py:239
  23.4 0.0 copy-done.2
  23.4 0.0 copy-done.7
  23.4 0.0 copy-done.1
  23.4 0.0 copy-done
  23.4 0.0 copy-done.8
  23.4 0.0 copy-done.3
  23.4 0.9 %dense.1 = (bf16[128,256]{1,0:T(8,128)(2,1)}, bf16[8,4,16,128]{3,2,1,0:T(8,128)(2,1)S(1)}) custom-call(bf16[8,4,16,128]{3,2,1,0:T(8,128)(2,1)S(1)} %bitcast.4, bf16[128,128]{1,0:T(8,128)(2,1)S(1)} %copy-done.3, s32[1,128]{1,0:T(1,128)S(1)} %bitcast.7, bf16[128,256]{1,0:T(8,128)(2,1)S(1)} %copy-done, bf16[128,256]{1,0:T(8,128)(2,1)S(1)} %copy-done.1, ...), custom_call_target="tpu_custom_call" | custom-call | tf_op jit(solution)/shard_map/dense/pallas_call | solution.py:241
  24.3 10.1 %all_to_all.11.grads_ref = bf16[32,16,128]{2,1,0:T(8,128)(2,1)S(1)} all-to-all(bf16[32,16,128]{2,1,0:T(8,128)(2,1)S(1)} %bitcast.5), channel_id=1, replica_groups=mesh['feat'=8,'col'=4] {'feat','col'}, dimensions={0} | all-to-all | bytes 262144 | tf_op jit(solution)/shard_map/all_to_all | solution.py:262
  34.4 0.0 copy-done.6
  34.4 0.0 copy-done.5
  34.4 0.0 copy-done.4
  34.4 2.7 %backward.1 = bf16[16,4096]{1,0:T(8,128)(2,1)} custom-call(s32[32]{0:T(128)S(1)} %copy-done.6, s32[256]{0:T(256)S(1)} %copy-done.4, s32[256]{0:T(256)S(1)} %copy-done.5, s32[1]{0:T(128)S(6)} %copy.14.count_hbm.count_ref, bf16[32,16,128]{2,1,0:T(8,128)(2,1)S(1)} %all_to_all.11.grads_ref, bf16[256,128,128]{2,1,0:T(8,128)(2,1)S(1)} %get-tuple-element.9.tiles_ref), custom_call_target="tpu_custom_call" | custom-call | tf_op jit(solution)/shard_map/backward/pallas_call | solution.py:270
Async XLA Ops:
  0.6 33.8 %copy-start.6 = (s32[32]{0:T(128)S(1)}, s32[32]{0:T(128)}, u32[]{:S(2)}) copy-start(s32[32]{0:T(128)} %order_ref.1) | copy-start | bytes 388
  0.6 33.8 %copy-start.5 = (s32[256]{0:T(256)S(1)}, s32[256]{0:T(256)}, u32[]{:S(2)}) copy-start(s32[256]{0:T(256)} %cols_ref.1) | copy-start | bytes 3076
  0.7 33.8 %copy-start.4 = (s32[256]{0:T(256)S(1)}, s32[256]{0:T(256)}, u32[]{:S(2)}) copy-start(s32[256]{0:T(256)} %rows_ref.1) | copy-start | bytes 3076
  0.7 22.7 %copy-start.2 = (bf16[128,256]{1,0:T(8,128)(2,1)S(1)}, bf16[128,256]{1,0:T(8,128)(2,1)}, u32[]{:S(2)}) copy-start(bf16[128,256]{1,0:T(8,128)(2,1)} %upstream_ref.1) | copy-start | bytes 196612
  0.7 22.7 %copy-start.7 = (f32[256]{0:T(256)S(1)}, f32[256]{0:T(256)}, u32[]{:S(2)}) copy-start(f32[256]{0:T(256)} %param.22) | copy-start | bytes 3076
  0.7 22.7 %copy-start.1 = (bf16[128,256]{1,0:T(8,128)(2,1)S(1)}, bf16[128,256]{1,0:T(8,128)(2,1)}, u32[]{:S(2)}) copy-start(bf16[128,256]{1,0:T(8,128)(2,1)} %w_neigh_ref.1) | copy-start | bytes 196612
  0.7 22.7 %copy-start = (bf16[128,256]{1,0:T(8,128)(2,1)S(1)}, bf16[128,256]{1,0:T(8,128)(2,1)}, u32[]{:S(2)}) copy-start(bf16[128,256]{1,0:T(8,128)(2,1)} %w_self_ref.1) | copy-start | bytes 196612
  0.7 22.7 %copy-start.8 = (s32[128]{0:T(128)S(1)}, s32[128]{0:T(128)}, u32[]{:S(2)}) copy-start(s32[128]{0:T(128)} %param.19) | copy-start | bytes 1540
  0.7 22.7 %copy-start.3 = (bf16[128,128]{1,0:T(8,128)(2,1)S(1)}, bf16[128,128]{1,0:T(8,128)(2,1)}, u32[]{:S(2)}) copy-start(bf16[128,128]{1,0:T(8,128)(2,1)} %self_ref.1) | copy-start | bytes 98308

commit v3 on v2

--- a/solution.py
+++ b/solution.py
@@ -43,7 +43,7 @@
     rows_hbm,
     cols_hbm,
     count_hbm,
-    feats_hbm,
+    feats_ref,
     tiles_hbm,
     partial_ref,
     tiles_ref,
@@ -51,7 +51,6 @@
     rows_ref,
     cols_ref,
     count_ref,
-    feats_ref,
     places,
     small_sems,
     sems,
@@ -67,7 +66,6 @@
             (rows_hbm, rows_ref),
             (cols_hbm, cols_ref),
             (count_hbm, count_ref),
-            (feats_hbm, feats_ref),
         ],
         small_sems,
     )
@@ -222,19 +220,22 @@
             jax.ShapeDtypeStruct((blocks_total, slice_width, tile_size), jnp.bfloat16),
             pltpu.VMEM(tiles.shape, tiles.dtype),
         ),
-        in_specs=[ANY] * 6,
+        in_specs=[ANY] * 4 + [VMEM, ANY],
         out_specs=(VMEM, VMEM),
         scratch_shapes=index_scratch
         + [
-            pltpu.VMEM(neighbour_feats.shape, neighbour_feats.dtype),
             pltpu.SMEM((blocks_total,), jnp.int32),
-            pltpu.SemaphoreType.DMA((5,)),
+            pltpu.SemaphoreType.DMA((4,)),
             pltpu.SemaphoreType.DMA((slots // CHUNK,)),
         ]
         + [pltpu.VMEM((blocks_total // ncol + 1, slice_width, tile_size), jnp.float32)] * ncol,
         compiler_params=params,
         name="forward",
-    )(*index_arrays, in_hbm(neighbour_feats), in_hbm(tiles))
+    )(
+        *index_arrays,
+        pltpu.with_memory_space_constraint(neighbour_feats, pltpu.VMEM),
+        in_hbm(tiles),
+    )
 
     got = lax.all_to_all(partial_value, ("feat", "col"), split_axis=0, concat_axis=0, tiled=True)
 

time: 37.3 us -> 36.2 us (0.971)
  Pallas kernels: 10 us -> 8.13 us
  local copies, waits for them, and re-layouts: 0.04 us -> 0.93 us
    pallas_call x1, Pallas kernels: 6.41 us -> 4.55 us  [local(): pl.pallas_call(forward_kernel, out_shape=(jax.ShapeDtypeStruct((blocks_to...]
    unnamed x18 -> x20, local copies, waits for them, and re-layouts: 0.04 us -> 0.93 us
where the time goes in v3:
time: 36.2 us; the launch traced here: 36.1 us
  blocking collectives  25.6 us (71%)
  Pallas kernels  8.13 us (22%)
  between operations  1.39 us (4%)
  local copies, waits for them, and re-layouts  0.93 us (3%)
    all_to_all x1, blocking collectives, local(): lax.all_to_all(partial_value, ('feat', 'col'), split_axis=0, concat_axis=...  15.5 us
    all_to_all x1, blocking collectives, local(): lax.all_to_all(back.reshape(blocks_total, slice_width, tile_size), ('feat...  10.1 us
    pallas_call x1, Pallas kernels, local(): pl.pallas_call(forward_kernel, out_shape=(jax.ShapeDtypeStruct((blocks_to...  4.55 us
    pallas_call x1, Pallas kernels, local(): pl.pallas_call(backward_kernel, out_shape=jax.ShapeDtypeStruct(neighbour_...  2.67 us
    unnamed x20, local copies, waits for them, and re-layouts  0.93 us
    pallas_call x1, Pallas kernels, local(): pl.pallas_call(dense_kernel, out_shape=(jax.ShapeDtypeStruct(upstream.sha...  0.9 us

profile of v3, /device:TPU:0, one launch (start us, length us, event | category | flops | bytes accessed | tf_op | source)
XLA Modules:
  0.0 36.1 jit_solution(8843864354777741929)
XLA Ops:
  0.6 0.0 copy-start.7
  0.6 0.0 copy-start.5
  1.3 0.0 copy-start
  1.3 0.9 %copy-done = bf16[16,4096]{1,0:T(8,128)(2,1)S(1)} copy-done((bf16[16,4096]{1,0:T(8,128)(2,1)S(1)}, bf16[16,4096]{1,0:T(8,128)(2,1)}, u32[]{:S(2)}) %copy-start) | copy-done | bytes 131096
  2.2 0.0 copy-start.1
  2.2 0.0 copy-start.2
  2.2 0.0 copy-start.3
  2.2 0.0 copy-start.8
  2.2 0.0 copy-start.9
  2.3 0.0 copy-start.6
  2.3 4.6 %forward.1 = (bf16[32,16,128]{2,1,0:T(8,128)(2,1)S(1)}, bf16[256,128,128]{2,1,0:T(8,128)(2,1)S(1)}) custom-call(s32[32]{0:T(128)} %order_ref.1, s32[256]{0:T(256)} %rows_ref.1, s32[256]{0:T(256)} %cols_ref.1, s32[1]{0:T(128)S(6)} %copy.14.count_hbm.count_ref, bf16[16,4096]{1,0:T(8,128)(2,1)S(1)} %copy-done, bf16[256,128,128]{2,1,0:T(8,128)(2,1)} %tiles_hbm.1), custom_call_target="tpu_custom_call" | custom-call | tf_op jit(solution)/shard_map/forward/pallas_call | solution.py:217
  6.8 15.5 %all_to_all.10 = bf16[32,16,128]{2,1,0:T(8,128)(2,1)S(1)} all-to-all(bf16[32,16,128]{2,1,0:T(8,128)(2,1)S(1)} %get-tuple-element.6), channel_id=1, replica_groups=mesh['feat'=8,'col'=4] {'feat','col'}, dimensions={0} | all-to-all | bytes 262144 | tf_op jit(solution)/shard_map/all_to_all | solution.py:240
  22.4 0.0 copy-done.1
  22.4 0.0 copy-done.2
  22.4 0.0 copy-done.3
  22.4 0.0 copy-done.4
  22.4 0.0 copy-done.8
  22.4 0.0 copy-done.9
  22.4 0.9 %dense.1 = (bf16[128,256]{1,0:T(8,128)(2,1)}, bf16[8,4,16,128]{3,2,1,0:T(8,128)(2,1)S(1)}) custom-call(bf16[8,4,16,128]{3,2,1,0:T(8,128)(2,1)S(1)} %bitcast.4, bf16[128,128]{1,0:T(8,128)(2,1)S(1)} %copy-done.4, s32[1,128]{1,0:T(1,128)S(1)} %bitcast.7, bf16[128,256]{1,0:T(8,128)(2,1)S(1)} %copy-done.1, bf16[128,256]{1,0:T(8,128)(2,1)S(1)} %copy-done.2, ...), custom_call_target="tpu_custom_call" | custom-call | tf_op jit(solution)/shard_map/dense/pallas_call | solution.py:242
  23.3 10.1 %all_to_all.11.grads_ref = bf16[32,16,128]{2,1,0:T(8,128)(2,1)S(1)} all-to-all(bf16[32,16,128]{2,1,0:T(8,128)(2,1)S(1)} %bitcast.5), channel_id=1, replica_groups=mesh['feat'=8,'col'=4] {'feat','col'}, dimensions={0} | all-to-all | bytes 262144 | tf_op jit(solution)/shard_map/all_to_all | solution.py:263
  33.4 0.0 copy-done.7
  33.4 0.0 copy-done.5
  33.4 0.0 copy-done.6
  33.4 2.7 %backward.1 = bf16[16,4096]{1,0:T(8,128)(2,1)} custom-call(s32[32]{0:T(128)S(1)} %copy-done.7, s32[256]{0:T(256)S(1)} %copy-done.5, s32[256]{0:T(256)S(1)} %copy-done.6, s32[1]{0:T(128)S(6)} %copy.14.count_hbm.count_ref, bf16[32,16,128]{2,1,0:T(8,128)(2,1)S(1)} %all_to_all.11.grads_ref, bf16[256,128,128]{2,1,0:T(8,128)(2,1)S(1)} %get-tuple-element.9.tiles_ref), custom_call_target="tpu_custom_call" | custom-call | tf_op jit(solution)/shard_map/backward/pallas_call | solution.py:271
  (1 shorter events, 0.0 us)
Async XLA Ops:
  0.6 32.8 %copy-start.7 = (s32[32]{0:T(128)S(1)}, s32[32]{0:T(128)}, u32[]{:S(2)}) copy-start(s32[32]{0:T(128)} %order_ref.1) | copy-start | bytes 388
  0.6 32.8 %copy-start.5 = (s32[256]{0:T(256)S(1)}, s32[256]{0:T(256)}, u32[]{:S(2)}) copy-start(s32[256]{0:T(256)} %rows_ref.1) | copy-start | bytes 3076
  1.3 0.9 %copy-start = (bf16[16,4096]{1,0:T(8,128)(2,1)S(1)}, bf16[16,4096]{1,0:T(8,128)(2,1)}, u32[]{:S(2)}) copy-start(bf16[16,4096]{1,0:T(8,128)(2,1)} %feats_ref.1) | copy-start | bytes 393220
  2.2 20.1 %copy-start.1 = (bf16[128,256]{1,0:T(8,128)(2,1)S(1)}, bf16[128,256]{1,0:T(8,128)(2,1)}, u32[]{:S(2)}) copy-start(bf16[128,256]{1,0:T(8,128)(2,1)} %w_self_ref.1) | copy-start | bytes 196612
  2.2 20.1 %copy-start.2 = (bf16[128,256]{1,0:T(8,128)(2,1)S(1)}, bf16[128,256]{1,0:T(8,128)(2,1)}, u32[]{:S(2)}) copy-start(bf16[128,256]{1,0:T(8,128)(2,1)} %w_neigh_ref.1) | copy-start | bytes 196612
  2.2 20.1 %copy-start.3 = (bf16[128,256]{1,0:T(8,128)(2,1)S(1)}, bf16[128,256]{1,0:T(8,128)(2,1)}, u32[]{:S(2)}) copy-start(bf16[128,256]{1,0:T(8,128)(2,1)} %upstream_ref.1) | copy-start | bytes 196612
  2.2 20.1 %copy-start.4 = (bf16[128,128]{1,0:T(8,128)(2,1)S(1)}, bf16[128,128]{1,0:T(8,128)(2,1)}, u32[]{:S(2)}) copy-start(bf16[128,128]{1,0:T(8,128)(2,1)} %self_ref.1) | copy-start | bytes 98308
  2.2 20.2 %copy-start.8 = (f32[256]{0:T(256)S(1)}, f32[256]{0:T(256)}, u32[]{:S(2)}) copy-start(f32[256]{0:T(256)} %param.22) | copy-start | bytes 3076
  2.2 20.2 %copy-start.9 = (s32[128]{0:T(128)S(1)}, s32[128]{0:T(128)}, u32[]{:S(2)}) copy-start(s32[128]{0:T(128)} %param.19) | copy-start | bytes 1540
  2.3 31.2 %copy-start.6 = (s32[256]{0:T(256)S(1)}, s32[256]{0:T(256)}, u32[]{:S(2)}) copy-start(s32[256]{0:T(256)} %cols_ref.1) | copy-start | bytes 3076

commit v4 on v2

--- a/solution.py
+++ b/solution.py
@@ -52,6 +52,7 @@
     cols_ref,
     count_ref,
     feats_ref,
+    feat_blocks,
     places,
     small_sems,
     sems,
@@ -72,11 +73,13 @@
         small_sems,
     )
     for chunk in range(slots // CHUNK):
-        tile_copy(tiles_hbm, tiles_ref, sems, chunk).start()
+        tile_copy(tiles_hbm, tiles_ref, sems, chunk).start(priority=1)
     for acc in accs:
         acc[...] = jnp.zeros_like(acc)
     for copy in small:
         copy.wait()
+    for block in range(feat_blocks.shape[0]):
+        feat_blocks[block] = feats_ref[:, block * tile_size : (block + 1) * tile_size]
     invert_order(order_ref, places)
     count = count_ref[0]
     zero, one, two = (jnp.asarray(v, tiles_ref.dtype) for v in (0, 1, 2))
@@ -85,10 +88,7 @@
         if first % CHUNK == 0:
             tile_copy(tiles_hbm, tiles_ref, sems, first // CHUNK).wait()
         pair = (first, first + 1)
-        feats = [
-            feats_ref[:, pl.ds(pl.multiple_of(cols_ref[slot] * tile_size, tile_size), tile_size)]
-            for slot in pair
-        ]
+        feats = [feat_blocks[cols_ref[slot]] for slot in pair]
         packed = (tiles_ref[first] + two * tiles_ref[first + 1]).T
         odd = jnp.where(packed >= two, one, zero)
         even = packed - two * odd
@@ -227,6 +227,7 @@
         scratch_shapes=index_scratch
         + [
             pltpu.VMEM(neighbour_feats.shape, neighbour_feats.dtype),
+            pltpu.VMEM((col_blocks, slice_width, tile_size), neighbour_feats.dtype),
             pltpu.SMEM((blocks_total,), jnp.int32),
             pltpu.SemaphoreType.DMA((5,)),
             pltpu.SemaphoreType.DMA((slots // CHUNK,)),

time: 37.3 us -> 35.3 us (0.946)
  Pallas kernels: 10 us -> 7.95 us
    pallas_call x1, Pallas kernels: 6.41 us -> 4.41 us  [local(): pl.pallas_call(forward_kernel, out_shape=(jax.ShapeDtypeStruct((blocks_to...]
where the time goes in v4:
time: 35.3 us; the launch traced here: 35.1 us
  blocking collectives  25.6 us (73%)
  Pallas kernels  7.95 us (23%)
  between operations  1.49 us (4%)
    all_to_all x1, blocking collectives, local(): lax.all_to_all(partial_value, ('feat', 'col'), split_axis=0, concat_axis=...  15.5 us
    all_to_all x1, blocking collectives, local(): lax.all_to_all(back.reshape(blocks_total, slice_width, tile_size), ('feat...  10.1 us
    pallas_call x1, Pallas kernels, local(): pl.pallas_call(forward_kernel, out_shape=(jax.ShapeDtypeStruct((blocks_to...  4.41 us
    pallas_call x1, Pallas kernels, local(): pl.pallas_call(backward_kernel, out_shape=jax.ShapeDtypeStruct(neighbour_...  2.64 us
    pallas_call x1, Pallas kernels, local(): pl.pallas_call(dense_kernel, out_shape=(jax.ShapeDtypeStruct(upstream.sha...  0.9 us

profile of v4, /device:TPU:0, one launch (start us, length us, event | category | flops | bytes accessed | tf_op | source)
XLA Modules:
  0.0 35.1 jit_solution(10502125522758256130)
XLA Ops:
  0.6 0.0 copy-start.6
  0.6 0.0 copy-start.5
  0.7 0.0 copy-start.4
  0.7 0.0 copy-start.2
  0.7 0.0 copy-start.7
  0.7 0.0 copy-start.1
  0.7 0.0 copy-start
  0.7 0.0 copy-start.8
  0.7 0.0 copy-start.3
  1.5 4.4 %forward.1 = (bf16[32,16,128]{2,1,0:T(8,128)(2,1)S(1)}, bf16[256,128,128]{2,1,0:T(8,128)(2,1)S(1)}) custom-call(s32[32]{0:T(128)} %order_ref.1, s32[256]{0:T(256)} %rows_ref.1, s32[256]{0:T(256)} %cols_ref.1, s32[1]{0:T(128)S(6)} %copy.14.count_hbm.count_ref, bf16[16,4096]{1,0:T(8,128)(2,1)} %feats_hbm.1, bf16[256,128,128]{2,1,0:T(8,128)(2,1)} %tiles_hbm.1), custom_call_target="tpu_custom_call" | custom-call | tf_op jit(solution)/shard_map/forward/pallas_call | solution.py:219
  5.9 15.5 %all_to_all.10 = bf16[32,16,128]{2,1,0:T(8,128)(2,1)S(1)} all-to-all(bf16[32,16,128]{2,1,0:T(8,128)(2,1)S(1)} %get-tuple-element.6), channel_id=1, replica_groups=mesh['feat'=8,'col'=4] {'feat','col'}, dimensions={0} | all-to-all | bytes 262144 | tf_op jit(solution)/shard_map/all_to_all | solution.py:240
  21.4 0.0 copy-done.2
  21.4 0.0 copy-done.7
  21.4 0.0 copy-done.1
  21.4 0.0 copy-done
  21.4 0.0 copy-done.8
  21.4 0.0 copy-done.3
  21.4 0.9 %dense.1 = (bf16[128,256]{1,0:T(8,128)(2,1)}, bf16[8,4,16,128]{3,2,1,0:T(8,128)(2,1)S(1)}) custom-call(bf16[8,4,16,128]{3,2,1,0:T(8,128)(2,1)S(1)} %bitcast.4, bf16[128,128]{1,0:T(8,128)(2,1)S(1)} %copy-done.3, s32[1,128]{1,0:T(1,128)S(1)} %bitcast.7, bf16[128,256]{1,0:T(8,128)(2,1)S(1)} %copy-done, bf16[128,256]{1,0:T(8,128)(2,1)S(1)} %copy-done.1, ...), custom_call_target="tpu_custom_call" | custom-call | tf_op jit(solution)/shard_map/dense/pallas_call | solution.py:242
  22.3 10.1 %all_to_all.11.grads_ref = bf16[32,16,128]{2,1,0:T(8,128)(2,1)S(1)} all-to-all(bf16[32,16,128]{2,1,0:T(8,128)(2,1)S(1)} %bitcast.5), channel_id=1, replica_groups=mesh['feat'=8,'col'=4] {'feat','col'}, dimensions={0} | all-to-all | bytes 262144 | tf_op jit(solution)/shard_map/all_to_all | solution.py:263
  32.4 0.0 copy-done.6
  32.4 0.0 copy-done.5
  32.4 0.0 copy-done.4
  32.5 2.6 %backward.1 = bf16[16,4096]{1,0:T(8,128)(2,1)} custom-call(s32[32]{0:T(128)S(1)} %copy-done.6, s32[256]{0:T(256)S(1)} %copy-done.4, s32[256]{0:T(256)S(1)} %copy-done.5, s32[1]{0:T(128)S(6)} %copy.14.count_hbm.count_ref, bf16[32,16,128]{2,1,0:T(8,128)(2,1)S(1)} %all_to_all.11.grads_ref, bf16[256,128,128]{2,1,0:T(8,128)(2,1)S(1)} %get-tuple-element.9.tiles_ref), custom_call_target="tpu_custom_call" | custom-call | tf_op jit(solution)/shard_map/backward/pallas_call | solution.py:271
Async XLA Ops:
  0.6 31.8 %copy-start.6 = (s32[32]{0:T(128)S(1)}, s32[32]{0:T(128)}, u32[]{:S(2)}) copy-start(s32[32]{0:T(128)} %order_ref.1) | copy-start | bytes 388
  0.6 31.8 %copy-start.5 = (s32[256]{0:T(256)S(1)}, s32[256]{0:T(256)}, u32[]{:S(2)}) copy-start(s32[256]{0:T(256)} %cols_ref.1) | copy-start | bytes 3076
  0.7 31.8 %copy-start.4 = (s32[256]{0:T(256)S(1)}, s32[256]{0:T(256)}, u32[]{:S(2)}) copy-start(s32[256]{0:T(256)} %rows_ref.1) | copy-start | bytes 3076
  0.7 20.7 %copy-start.2 = (bf16[128,256]{1,0:T(8,128)(2,1)S(1)}, bf16[128,256]{1,0:T(8,128)(2,1)}, u32[]{:S(2)}) copy-start(bf16[128,256]{1,0:T(8,128)(2,1)} %upstream_ref.1) | copy-start | bytes 196612
  0.7 20.7 %copy-start.7 = (f32[256]{0:T(256)S(1)}, f32[256]{0:T(256)}, u32[]{:S(2)}) copy-start(f32[256]{0:T(256)} %param.22) | copy-start | bytes 3076
  0.7 20.7 %copy-start.1 = (bf16[128,256]{1,0:T(8,128)(2,1)S(1)}, bf16[128,256]{1,0:T(8,128)(2,1)}, u32[]{:S(2)}) copy-start(bf16[128,256]{1,0:T(8,128)(2,1)} %w_neigh_ref.1) | copy-start | bytes 196612
  0.7 20.7 %copy-start = (bf16[128,256]{1,0:T(8,128)(2,1)S(1)}, bf16[128,256]{1,0:T(8,128)(2,1)}, u32[]{:S(2)}) copy-start(bf16[128,256]{1,0:T(8,128)(2,1)} %w_self_ref.1) | copy-start | bytes 196612
  0.7 20.7 %copy-start.8 = (s32[128]{0:T(128)S(1)}, s32[128]{0:T(128)}, u32[]{:S(2)}) copy-start(s32[128]{0:T(128)} %param.19) | copy-start | bytes 1540
  0.7 20.7 %copy-start.3 = (bf16[128,128]{1,0:T(8,128)(2,1)S(1)}, bf16[128,128]{1,0:T(8,128)(2,1)}, u32[]{:S(2)}) copy-start(bf16[128,128]{1,0:T(8,128)(2,1)} %self_ref.1) | copy-start | bytes 98308

commit v5 on v4

--- a/solution.py
+++ b/solution.py
@@ -150,13 +150,18 @@
     count_ref,
     grads_ref,
     tiles_ref,
+    hidden_ref,
     out_ref,
+    hidden_hbm,
     places,
     acc_even,
     acc_odd,
+    hidden_sem,
 ):
     slots, tile_size, _ = tiles_ref.shape
     slice_width = out_ref.shape[0]
+    leaving = pltpu.make_async_copy(hidden_ref, hidden_hbm, hidden_sem)
+    leaving.start()
     invert_order(order_ref, places)
     accs = (acc_even, acc_odd)
     for acc in accs:
@@ -179,6 +184,7 @@
     for block in range(col_blocks):
         total = acc_even[block] + acc_odd[block]
         out_ref[:, block * tile_size : (block + 1) * tile_size] = total.astype(out_ref.dtype)
+    leaving.wait()
 
 
 VMEM = pl.BlockSpec(memory_space=pltpu.VMEM)
@@ -239,10 +245,10 @@
 
     got = lax.all_to_all(partial_value, ("feat", "col"), split_axis=0, concat_axis=0, tiled=True)
 
-    hidden_out, back = pl.pallas_call(
+    hidden, back = pl.pallas_call(
         dense_kernel,
         out_shape=(
-            jax.ShapeDtypeStruct(upstream.shape, jnp.bfloat16),
+            pltpu.VMEM(upstream.shape, jnp.bfloat16),
             jax.ShapeDtypeStruct((nfeat, ncol, slice_width, tile_size), jnp.bfloat16),
         ),
         in_specs=[VMEM] * 7,
@@ -268,15 +274,19 @@
         tiled=True,
     )
 
-    neigh_grad = pl.pallas_call(
+    neigh_grad, hidden_out = pl.pallas_call(
         backward_kernel,
-        out_shape=jax.ShapeDtypeStruct(neighbour_feats.shape, jnp.bfloat16),
-        in_specs=[SMEM] * 4 + [VMEM] * 2,
-        out_specs=VMEM,
+        out_shape=(
+            jax.ShapeDtypeStruct(neighbour_feats.shape, jnp.bfloat16),
+            jax.ShapeDtypeStruct(upstream.shape, jnp.bfloat16),
+        ),
+        in_specs=[SMEM] * 4 + [VMEM] * 3,
+        out_specs=(VMEM, ANY),
         scratch_shapes=[
             pltpu.SMEM((blocks_total,), jnp.int32),
             pltpu.VMEM((col_blocks + 1, slice_width, tile_size), jnp.float32),
             pltpu.VMEM((col_blocks + 1, slice_width, tile_size), jnp.float32),
+            pltpu.SemaphoreType.DMA,
         ],
         compiler_params=params,
         name="backward",
@@ -287,6 +297,7 @@
         tile_count,
         row_grads,
         pltpu.with_memory_space_constraint(tiles_kept, pltpu.VMEM),
+        pltpu.with_memory_space_constraint(hidden, pltpu.VMEM),
     )
     return (hidden_out, neigh_grad)
 

time: 35.3 us -> 35 us (level)
  no operation moved by 1% of the time
where the time goes in v5:
time: 35 us; the launch traced here: 34.8 us
  blocking collectives  25.6 us (73%)
  Pallas kernels  7.64 us (22%)
  between operations  1.49 us (4%)
    all_to_all x1, blocking collectives, local(): lax.all_to_all(partial_value, ('feat', 'col'), split_axis=0, concat_axis=...  15.5 us
    all_to_all x1, blocking collectives, local(): lax.all_to_all(back.reshape(blocks_total, slice_width, tile_size), ('feat...  10.1 us
    pallas_call x1, Pallas kernels, local(): pl.pallas_call(forward_kernel, out_shape=(jax.ShapeDtypeStruct((blocks_to...  4.42 us
    pallas_call x1, Pallas kernels, local(): pl.pallas_call(backward_kernel, out_shape=(jax.ShapeDtypeStruct(neighbour...  2.8 us

profile of v5, /device:TPU:0, one launch (start us, length us, event | category | flops | bytes accessed | tf_op | source)
XLA Modules:
  0.0 34.8 jit_solution(2498200213571087074)
XLA Ops:
  0.6 0.0 copy-start.6
  0.6 0.0 copy-start.5
  0.7 0.0 copy-start.4
  0.7 0.0 copy-start.2
  0.7 0.0 copy-start.7
  0.7 0.0 copy-start.1
  0.7 0.0 copy-start
  0.7 0.0 copy-start.8
  0.7 0.0 copy-start.3
  1.5 4.4 %forward.1 = (bf16[32,16,128]{2,1,0:T(8,128)(2,1)S(1)}, bf16[256,128,128]{2,1,0:T(8,128)(2,1)S(1)}) custom-call(s32[32]{0:T(128)} %order_ref.1, s32[256]{0:T(256)} %rows_ref.1, s32[256]{0:T(256)} %cols_ref.1, s32[1]{0:T(128)S(6)} %copy.14.count_hbm.count_ref, bf16[16,4096]{1,0:T(8,128)(2,1)} %feats_hbm.1, bf16[256,128,128]{2,1,0:T(8,128)(2,1)} %tiles_hbm.1), custom_call_target="tpu_custom_call" | custom-call | tf_op jit(solution)/shard_map/forward/pallas_call | solution.py:225
  5.9 15.5 %all_to_all.10 = bf16[32,16,128]{2,1,0:T(8,128)(2,1)S(1)} all-to-all(bf16[32,16,128]{2,1,0:T(8,128)(2,1)S(1)} %get-tuple-element.8), channel_id=1, replica_groups=mesh['feat'=8,'col'=4] {'feat','col'}, dimensions={0} | all-to-all | bytes 262144 | tf_op jit(solution)/shard_map/all_to_all | solution.py:246
  21.4 0.0 copy-done.2
  21.4 0.0 copy-done.7
  21.4 0.0 copy-done.1
  21.4 0.0 copy-done
  21.4 0.0 copy-done.8
  21.4 0.0 copy-done.3
  21.4 0.4 %dense.1 = (bf16[128,256]{1,0:T(8,128)(2,1)S(1)}, bf16[8,4,16,128]{3,2,1,0:T(8,128)(2,1)S(1)}) custom-call(bf16[8,4,16,128]{3,2,1,0:T(8,128)(2,1)S(1)} %bitcast.4, bf16[128,128]{1,0:T(8,128)(2,1)S(1)} %copy-done.3, s32[1,128]{1,0:T(1,128)S(1)} %bitcast.7, bf16[128,256]{1,0:T(8,128)(2,1)S(1)} %copy-done, bf16[128,256]{1,0:T(8,128)(2,1)S(1)} %copy-done.1, ...), custom_call_target="tpu_custom_call" | custom-call | tf_op jit(solution)/shard_map/dense/pallas_call | solution.py:248
  21.9 10.1 %all_to_all.11.grads_ref = bf16[32,16,128]{2,1,0:T(8,128)(2,1)S(1)} all-to-all(bf16[32,16,128]{2,1,0:T(8,128)(2,1)S(1)} %bitcast.5), channel_id=1, replica_groups=mesh['feat'=8,'col'=4] {'feat','col'}, dimensions={0} | all-to-all | bytes 262144 | tf_op jit(solution)/shard_map/all_to_all | solution.py:269
  32.0 0.0 copy-done.6
  32.0 0.0 copy-done.5
  32.0 0.0 copy-done.4
  32.0 2.8 %backward.1 = (bf16[16,4096]{1,0:T(8,128)(2,1)}, bf16[128,256]{1,0:T(8,128)(2,1)}) custom-call(s32[32]{0:T(128)S(1)} %copy-done.6, s32[256]{0:T(256)S(1)} %copy-done.4, s32[256]{0:T(256)S(1)} %copy-done.5, s32[1]{0:T(128)S(6)} %copy.14.count_hbm.count_ref, bf16[32,16,128]{2,1,0:T(8,128)(2,1)S(1)} %all_to_all.11.grads_ref, ...), custom_call_target="tpu_custom_call" | custom-call | tf_op jit(solution)/shard_map/backward/pallas_call | solution.py:277
Async XLA Ops:
  0.6 31.3 %copy-start.6 = (s32[32]{0:T(128)S(1)}, s32[32]{0:T(128)}, u32[]{:S(2)}) copy-start(s32[32]{0:T(128)} %order_ref.1) | copy-start | bytes 388
  0.6 31.3 %copy-start.5 = (s32[256]{0:T(256)S(1)}, s32[256]{0:T(256)}, u32[]{:S(2)}) copy-start(s32[256]{0:T(256)} %cols_ref.1) | copy-start | bytes 3076
  0.7 31.3 %copy-start.4 = (s32[256]{0:T(256)S(1)}, s32[256]{0:T(256)}, u32[]{:S(2)}) copy-start(s32[256]{0:T(256)} %rows_ref.1) | copy-start | bytes 3076
  0.7 20.7 %copy-start.2 = (bf16[128,256]{1,0:T(8,128)(2,1)S(1)}, bf16[128,256]{1,0:T(8,128)(2,1)}, u32[]{:S(2)}) copy-start(bf16[128,256]{1,0:T(8,128)(2,1)} %upstream_ref.1) | copy-start | bytes 196612
  0.7 20.7 %copy-start.7 = (f32[256]{0:T(256)S(1)}, f32[256]{0:T(256)}, u32[]{:S(2)}) copy-start(f32[256]{0:T(256)} %param.22) | copy-start | bytes 3076
  0.7 20.7 %copy-start.1 = (bf16[128,256]{1,0:T(8,128)(2,1)S(1)}, bf16[128,256]{1,0:T(8,128)(2,1)}, u32[]{:S(2)}) copy-start(bf16[128,256]{1,0:T(8,128)(2,1)} %w_neigh_ref.1) | copy-start | bytes 196612
  0.7 20.7 %copy-start = (bf16[128,256]{1,0:T(8,128)(2,1)S(1)}, bf16[128,256]{1,0:T(8,128)(2,1)}, u32[]{:S(2)}) copy-start(bf16[128,256]{1,0:T(8,128)(2,1)} %w_self_ref.1) | copy-start | bytes 196612
  0.7 20.7 %copy-start.8 = (s32[128]{0:T(128)S(1)}, s32[128]{0:T(128)}, u32[]{:S(2)}) copy-start(s32[128]{0:T(128)} %param.19) | copy-start | bytes 1540
  0.7 20.7 %copy-start.3 = (bf16[128,128]{1,0:T(8,128)(2,1)S(1)}, bf16[128,128]{1,0:T(8,128)(2,1)}, u32[]{:S(2)}) copy-start(bf16[128,128]{1,0:T(8,128)(2,1)} %self_ref.1) | copy-start | bytes 98308

commit v6 on v5

--- a/solution.py
+++ b/solution.py
@@ -1,3 +1,5 @@
+import functools
+
 import jax
 import jax.numpy as jnp
 from jax import lax
@@ -8,9 +10,9 @@
 CHUNK = 64
 
 
-def invert_order(order_ref, places):
+def invert_order(order_ref, places, value):
     def body(position, carry):
-        places[order_ref[position]] = position
+        places[order_ref[position]] = value(position)
         return carry
 
     lax.fori_loop(0, order_ref.shape[0], body, 0, unroll=8)
@@ -61,7 +63,7 @@
     slots, tile_size, _ = tiles_ref.shape
     blocks_total, slice_width, _ = partial_ref.shape
     ncol = len(accs)
-    spare = blocks_total // ncol
+    nfeat = blocks_total // ncol
     small = fetch(
         [
             (order_hbm, order_ref),
@@ -80,7 +82,7 @@
         copy.wait()
     for block in range(feat_blocks.shape[0]):
         feat_blocks[block] = feats_ref[:, block * tile_size : (block + 1) * tile_size]
-    invert_order(order_ref, places)
+    invert_order(order_ref, places, lambda position: position // ncol)
     count = count_ref[0]
     zero, one, two = (jnp.asarray(v, tiles_ref.dtype) for v in (0, 1, 2))
 
@@ -98,11 +100,11 @@
             preferred_element_type=jnp.float32,
         )
         for i, slot in enumerate(pair):
-            target = jnp.where(slot < count, places[rows_ref[slot]] // ncol, spare)
+            target = jnp.where(slot < count, places[rows_ref[slot]], nfeat)
             accs[slot % ncol][target] += pieces[i * slice_width : (i + 1) * slice_width]
 
-    for block in range(blocks_total):
-        partial_ref[block] = accs[block % ncol][block // ncol].astype(partial_ref.dtype)
+    for col, acc in enumerate(accs):
+        partial_ref[col * nfeat : (col + 1) * nfeat] = acc[:nfeat].astype(partial_ref.dtype)
 
 
 def dense_kernel(
@@ -117,11 +119,12 @@
     back_ref,
     summed,
 ):
-    nfeat, ncol, slice_width, tile_size = got_ref.shape
+    ncol, nfeat, slice_width, tile_size = got_ref.shape
     for f in range(nfeat):
-        summed[pl.ds(f * slice_width, slice_width), :] = jnp.sum(
-            got_ref[f].astype(jnp.float32), axis=0
-        )
+        total = got_ref[0, f].astype(jnp.float32)
+        for c in range(1, ncol):
+            total = total + got_ref[c, f].astype(jnp.float32)
+        summed[pl.ds(f * slice_width, slice_width), :] = total
     scale = lax.rsqrt(degree_ref[...].astype(jnp.float32))
     aggregate = (summed[...] * scale).astype(jnp.bfloat16)
     pre = jnp.dot(self_ref[...], w_self_ref[...], preferred_element_type=jnp.float32)
@@ -140,10 +143,11 @@
     for f in range(nfeat):
         piece = back[f * slice_width : (f + 1) * slice_width].astype(jnp.bfloat16)
         for c in range(ncol):
-            back_ref[f, c] = piece
+            back_ref[c, f] = piece
 
 
 def backward_kernel(
+    ncol,
     order_ref,
     rows_ref,
     cols_ref,
@@ -160,9 +164,12 @@
 ):
     slots, tile_size, _ = tiles_ref.shape
     slice_width = out_ref.shape[0]
+    nfeat = grads_ref.shape[0] // ncol
     leaving = pltpu.make_async_copy(hidden_ref, hidden_hbm, hidden_sem)
     leaving.start()
-    invert_order(order_ref, places)
+    invert_order(
+        order_ref, places, lambda position: position % ncol * nfeat + position // ncol
+    )
     accs = (acc_even, acc_odd)
     for acc in accs:
         acc[...] = jnp.zeros_like(acc)
@@ -243,13 +250,13 @@
         name="forward",
     )(*index_arrays, in_hbm(neighbour_feats), in_hbm(tiles))
 
-    got = lax.all_to_all(partial_value, ("feat", "col"), split_axis=0, concat_axis=0, tiled=True)
+    got = lax.all_to_all(partial_value, ("col", "feat"), split_axis=0, concat_axis=0, tiled=True)
 
     hidden, back = pl.pallas_call(
         dense_kernel,
         out_shape=(
             pltpu.VMEM(upstream.shape, jnp.bfloat16),
-            jax.ShapeDtypeStruct((nfeat, ncol, slice_width, tile_size), jnp.bfloat16),
+            jax.ShapeDtypeStruct((ncol, nfeat, slice_width, tile_size), jnp.bfloat16),
         ),
         in_specs=[VMEM] * 7,
         out_specs=(VMEM, VMEM),
@@ -257,7 +264,7 @@
         compiler_params=params,
         name="dense",
     )(
-        got.reshape(nfeat, ncol, slice_width, tile_size),
+        got.reshape(ncol, nfeat, slice_width, tile_size),
         self_feats,
         degree.reshape(1, rows),
         w_self,
@@ -268,14 +275,14 @@
 
     row_grads = lax.all_to_all(
         back.reshape(blocks_total, slice_width, tile_size),
-        ("feat", "col"),
+        ("col", "feat"),
         split_axis=0,
         concat_axis=0,
         tiled=True,
     )
 
     neigh_grad, hidden_out = pl.pallas_call(
-        backward_kernel,
+        functools.partial(backward_kernel, ncol),
         out_shape=(
             jax.ShapeDtypeStruct(neighbour_feats.shape, jnp.bfloat16),
             jax.ShapeDtypeStruct(upstream.shape, jnp.bfloat16),

time: 35 us -> 34.5 us (0.986)
  blocking collectives: 25.6 us -> 25.2 us
    all_to_all x2, blocking collectives: 25.6 us -> 25.2 us  [the longest x1 15.3 us: local(): lax.all_to_all(partial_value, ('col', 'feat'), split_axis=0, concat_axis=...]
where the time goes in v6:
time: 34.5 us; the launch traced here: 34.3 us
  blocking collectives  25.2 us (73%)
  Pallas kernels  7.63 us (22%)
  between operations  1.49 us (4%)
    all_to_all x1, blocking collectives, local(): lax.all_to_all(partial_value, ('col', 'feat'), split_axis=0, concat_axis=...  15.3 us
    all_to_all x1, blocking collectives, local(): lax.all_to_all(back.reshape(blocks_total, slice_width, tile_size), ('col'...  9.88 us
    pallas_call x1, Pallas kernels, local(): pl.pallas_call(forward_kernel, out_shape=(jax.ShapeDtypeStruct((blocks_to...  4.18 us
    pallas_call x1, Pallas kernels, local(): pl.pallas_call(functools.partial(backward_kernel, ncol), out_shape=(jax.S...  3.02 us

profile of v6, /device:TPU:0, one launch (start us, length us, event | category | flops | bytes accessed | tf_op | source)
XLA Modules:
  0.0 34.3 jit_solution(16811009736339997073)
XLA Ops:
  0.6 0.0 copy-start.6
  0.6 0.0 copy-start.5
  0.7 0.0 copy-start.4
  0.7 0.0 copy-start.2
  0.7 0.0 copy-start.7
  0.7 0.0 copy-start.1
  0.7 0.0 copy-start
  0.7 0.0 copy-start.8
  0.7 0.0 copy-start.3
  1.5 4.2 %forward.1 = (bf16[32,16,128]{2,1,0:T(8,128)(2,1)S(1)}, bf16[256,128,128]{2,1,0:T(8,128)(2,1)S(1)}) custom-call(s32[32]{0:T(128)} %order_ref.1, s32[256]{0:T(256)} %rows_ref.1, s32[256]{0:T(256)} %cols_ref.1, s32[1]{0:T(128)S(6)} %copy.14.count_hbm.count_ref, bf16[16,4096]{1,0:T(8,128)(2,1)} %feats_hbm.1, bf16[256,128,128]{2,1,0:T(8,128)(2,1)} %tiles_hbm.1), custom_call_target="tpu_custom_call" | custom-call | tf_op jit(solution)/shard_map/forward/pallas_call | solution.py:232
  5.7 15.3 %all_to_all.10 = bf16[32,16,128]{2,1,0:T(8,128)(2,1)S(1)} all-to-all(bf16[32,16,128]{2,1,0:T(8,128)(2,1)S(1)} %get-tuple-element.8), channel_id=1, replica_groups=mesh['feat'=8,'col'=4] {'col','feat'}, dimensions={0} | all-to-all | bytes 262144 | tf_op jit(solution)/shard_map/all_to_all | solution.py:253
  20.9 0.0 copy-done.2
  20.9 0.0 copy-done.7
  20.9 0.0 copy-done.1
  20.9 0.0 copy-done
  21.0 0.0 copy-done.8
  21.0 0.0 copy-done.3
  21.0 0.4 %dense.1 = (bf16[128,256]{1,0:T(8,128)(2,1)S(1)}, bf16[4,8,16,128]{3,2,1,0:T(8,128)(2,1)S(1)}) custom-call(bf16[4,8,16,128]{3,2,1,0:T(8,128)(2,1)S(1)} %bitcast.4, bf16[128,128]{1,0:T(8,128)(2,1)S(1)} %copy-done.3, s32[1,128]{1,0:T(1,128)S(1)} %bitcast.7, bf16[128,256]{1,0:T(8,128)(2,1)S(1)} %copy-done, bf16[128,256]{1,0:T(8,128)(2,1)S(1)} %copy-done.1, ...), custom_call_target="tpu_custom_call" | custom-call | tf_op jit(solution)/shard_map/dense/pallas_call | solution.py:255
  21.4 9.9 %all_to_all.11.grads_ref = bf16[32,16,128]{2,1,0:T(8,128)(2,1)S(1)} all-to-all(bf16[32,16,128]{2,1,0:T(8,128)(2,1)S(1)} %bitcast.5), channel_id=1, replica_groups=mesh['feat'=8,'col'=4] {'col','feat'}, dimensions={0} | all-to-all | bytes 262144 | tf_op jit(solution)/shard_map/all_to_all | solution.py:276
  31.3 0.0 copy-done.6
  31.3 0.0 copy-done.5
  31.3 0.0 copy-done.4
  31.3 3.0 %backward.1 = (bf16[16,4096]{1,0:T(8,128)(2,1)}, bf16[128,256]{1,0:T(8,128)(2,1)}) custom-call(s32[32]{0:T(128)S(1)} %copy-done.6, s32[256]{0:T(256)S(1)} %copy-done.4, s32[256]{0:T(256)S(1)} %copy-done.5, s32[1]{0:T(128)S(6)} %copy.14.count_hbm.count_ref, bf16[32,16,128]{2,1,0:T(8,128)(2,1)S(1)} %all_to_all.11.grads_ref, ...), custom_call_target="tpu_custom_call" | custom-call | tf_op jit(solution)/shard_map/backward/pallas_call | solution.py:284
Async XLA Ops:
  0.6 30.7 %copy-start.6 = (s32[32]{0:T(128)S(1)}, s32[32]{0:T(128)}, u32[]{:S(2)}) copy-start(s32[32]{0:T(128)} %order_ref.1) | copy-start | bytes 388
  0.6 30.7 %copy-start.5 = (s32[256]{0:T(256)S(1)}, s32[256]{0:T(256)}, u32[]{:S(2)}) copy-start(s32[256]{0:T(256)} %cols_ref.1) | copy-start | bytes 3076
  0.7 30.6 %copy-start.4 = (s32[256]{0:T(256)S(1)}, s32[256]{0:T(256)}, u32[]{:S(2)}) copy-start(s32[256]{0:T(256)} %rows_ref.1) | copy-start | bytes 3076
  0.7 20.3 %copy-start.2 = (bf16[128,256]{1,0:T(8,128)(2,1)S(1)}, bf16[128,256]{1,0:T(8,128)(2,1)}, u32[]{:S(2)}) copy-start(bf16[128,256]{1,0:T(8,128)(2,1)} %upstream_ref.1) | copy-start | bytes 196612
  0.7 20.3 %copy-start.7 = (f32[256]{0:T(256)S(1)}, f32[256]{0:T(256)}, u32[]{:S(2)}) copy-start(f32[256]{0:T(256)} %param.22) | copy-start | bytes 3076
  0.7 20.3 %copy-start.1 = (bf16[128,256]{1,0:T(8,128)(2,1)S(1)}, bf16[128,256]{1,0:T(8,128)(2,1)}, u32[]{:S(2)}) copy-start(bf16[128,256]{1,0:T(8,128)(2,1)} %w_neigh_ref.1) | copy-start | bytes 196612
  0.7 20.3 %copy-start = (bf16[128,256]{1,0:T(8,128)(2,1)S(1)}, bf16[128,256]{1,0:T(8,128)(2,1)}, u32[]{:S(2)}) copy-start(bf16[128,256]{1,0:T(8,128)(2,1)} %w_self_ref.1) | copy-start | bytes 196612
  0.7 20.3 %copy-start.8 = (s32[128]{0:T(128)S(1)}, s32[128]{0:T(128)}, u32[]{:S(2)}) copy-start(s32[128]{0:T(128)} %param.19) | copy-start | bytes 1540
  0.7 20.3 %copy-start.3 = (bf16[128,128]{1,0:T(8,128)(2,1)S(1)}, bf16[128,128]{1,0:T(8,128)(2,1)}, u32[]{:S(2)}) copy-start(bf16[128,128]{1,0:T(8,128)(2,1)} %self_ref.1) | copy-start | bytes 98308

commit v7 on v6

--- a/solution.py
+++ b/solution.py
@@ -10,12 +10,14 @@
 CHUNK = 64
 
 
-def invert_order(order_ref, places, value):
-    def body(position, carry):
-        places[order_ref[position]] = value(position)
+def invert_order(order_ref, places, ncol, value):
+    def body(feat, carry):
+        for col in range(ncol):
+            places[order_ref[feat * ncol + col]] = value(feat, col)
         return carry
 
-    lax.fori_loop(0, order_ref.shape[0], body, 0, unroll=8)
+    nfeat = order_ref.shape[0] // ncol
+    lax.fori_loop(0, nfeat, body, 0, unroll=max(1, 32 // ncol))
 
 
 def fetch(pairs, sems):
@@ -82,7 +84,7 @@
         copy.wait()
     for block in range(feat_blocks.shape[0]):
         feat_blocks[block] = feats_ref[:, block * tile_size : (block + 1) * tile_size]
-    invert_order(order_ref, places, lambda position: position // ncol)
+    invert_order(order_ref, places, ncol, lambda feat, col: feat)
     count = count_ref[0]
     zero, one, two = (jnp.asarray(v, tiles_ref.dtype) for v in (0, 1, 2))
 
@@ -167,9 +169,7 @@
     nfeat = grads_ref.shape[0] // ncol
     leaving = pltpu.make_async_copy(hidden_ref, hidden_hbm, hidden_sem)
     leaving.start()
-    invert_order(
-        order_ref, places, lambda position: position % ncol * nfeat + position // ncol
-    )
+    invert_order(order_ref, places, ncol, lambda feat, col: col * nfeat + feat)
     accs = (acc_even, acc_odd)
     for acc in accs:
         acc[...] = jnp.zeros_like(acc)

time: 34.5 us -> 34.7 us (level)
  no operation moved by 1% of the time
where the time goes in v7:
time: 34.7 us; the launch traced here: 34.5 us
  blocking collectives  25.2 us (73%)
  Pallas kernels  7.76 us (22%)
  between operations  1.49 us (4%)
    all_to_all x1, blocking collectives, local(): lax.all_to_all(partial_value, ('col', 'feat'), split_axis=0, concat_axis=...  15.3 us
    all_to_all x1, blocking collectives, local(): lax.all_to_all(back.reshape(blocks_total, slice_width, tile_size), ('col'...  9.88 us
    pallas_call x1, Pallas kernels, local(): pl.pallas_call(forward_kernel, out_shape=(jax.ShapeDtypeStruct((blocks_to...  4.18 us
    pallas_call x1, Pallas kernels, local(): pl.pallas_call(functools.partial(backward_kernel, ncol), out_shape=(jax.S...  3.15 us

profile of v7, /device:TPU:0, one launch (start us, length us, event | category | flops | bytes accessed | tf_op | source)
XLA Modules:
  0.0 34.5 jit_solution(3816284326876568635)
XLA Ops:
  0.6 0.0 copy-start.6
  0.6 0.0 copy-start.5
  0.7 0.0 copy-start.4
  0.7 0.0 copy-start.2
  0.7 0.0 copy-start.7
  0.7 0.0 copy-start.1
  0.7 0.0 copy-start
  0.7 0.0 copy-start.8
  0.7 0.0 copy-start.3
  1.5 4.2 %forward.1 = (bf16[32,16,128]{2,1,0:T(8,128)(2,1)S(1)}, bf16[256,128,128]{2,1,0:T(8,128)(2,1)S(1)}) custom-call(s32[32]{0:T(128)} %order_ref.1, s32[256]{0:T(256)} %rows_ref.1, s32[256]{0:T(256)} %cols_ref.1, s32[1]{0:T(128)S(6)} %copy.14.count_hbm.count_ref, bf16[16,4096]{1,0:T(8,128)(2,1)} %feats_hbm.1, bf16[256,128,128]{2,1,0:T(8,128)(2,1)} %tiles_hbm.1), custom_call_target="tpu_custom_call" | custom-call | tf_op jit(solution)/shard_map/forward/pallas_call | solution.py:232
  5.7 15.3 %all_to_all.10 = bf16[32,16,128]{2,1,0:T(8,128)(2,1)S(1)} all-to-all(bf16[32,16,128]{2,1,0:T(8,128)(2,1)S(1)} %get-tuple-element.8), channel_id=1, replica_groups=mesh['feat'=8,'col'=4] {'col','feat'}, dimensions={0} | all-to-all | bytes 262144 | tf_op jit(solution)/shard_map/all_to_all | solution.py:253
  20.9 0.0 copy-done.2
  20.9 0.0 copy-done.7
  20.9 0.0 copy-done.1
  21.0 0.0 copy-done
  21.0 0.0 copy-done.8
  21.0 0.0 copy-done.3
  21.0 0.4 %dense.1 = (bf16[128,256]{1,0:T(8,128)(2,1)S(1)}, bf16[4,8,16,128]{3,2,1,0:T(8,128)(2,1)S(1)}) custom-call(bf16[4,8,16,128]{3,2,1,0:T(8,128)(2,1)S(1)} %bitcast.4, bf16[128,128]{1,0:T(8,128)(2,1)S(1)} %copy-done.3, s32[1,128]{1,0:T(1,128)S(1)} %bitcast.7, bf16[128,256]{1,0:T(8,128)(2,1)S(1)} %copy-done, bf16[128,256]{1,0:T(8,128)(2,1)S(1)} %copy-done.1, ...), custom_call_target="tpu_custom_call" | custom-call | tf_op jit(solution)/shard_map/dense/pallas_call | solution.py:255
  21.4 9.9 %all_to_all.11.grads_ref = bf16[32,16,128]{2,1,0:T(8,128)(2,1)S(1)} all-to-all(bf16[32,16,128]{2,1,0:T(8,128)(2,1)S(1)} %bitcast.5), channel_id=1, replica_groups=mesh['feat'=8,'col'=4] {'col','feat'}, dimensions={0} | all-to-all | bytes 262144 | tf_op jit(solution)/shard_map/all_to_all | solution.py:276
  31.3 0.0 copy-done.6
  31.3 0.0 copy-done.5
  31.3 0.0 copy-done.4
  31.3 3.2 %backward.1 = (bf16[16,4096]{1,0:T(8,128)(2,1)}, bf16[128,256]{1,0:T(8,128)(2,1)}) custom-call(s32[32]{0:T(128)S(1)} %copy-done.6, s32[256]{0:T(256)S(1)} %copy-done.4, s32[256]{0:T(256)S(1)} %copy-done.5, s32[1]{0:T(128)S(6)} %copy.14.count_hbm.count_ref, bf16[32,16,128]{2,1,0:T(8,128)(2,1)S(1)} %all_to_all.11.grads_ref, ...), custom_call_target="tpu_custom_call" | custom-call | tf_op jit(solution)/shard_map/backward/pallas_call | solution.py:284
Async XLA Ops:
  0.6 30.7 %copy-start.6 = (s32[32]{0:T(128)S(1)}, s32[32]{0:T(128)}, u32[]{:S(2)}) copy-start(s32[32]{0:T(128)} %order_ref.1) | copy-start | bytes 388
  0.6 30.7 %copy-start.5 = (s32[256]{0:T(256)S(1)}, s32[256]{0:T(256)}, u32[]{:S(2)}) copy-start(s32[256]{0:T(256)} %cols_ref.1) | copy-start | bytes 3076
  0.7 30.7 %copy-start.4 = (s32[256]{0:T(256)S(1)}, s32[256]{0:T(256)}, u32[]{:S(2)}) copy-start(s32[256]{0:T(256)} %rows_ref.1) | copy-start | bytes 3076
  0.7 20.3 %copy-start.2 = (bf16[128,256]{1,0:T(8,128)(2,1)S(1)}, bf16[128,256]{1,0:T(8,128)(2,1)}, u32[]{:S(2)}) copy-start(bf16[128,256]{1,0:T(8,128)(2,1)} %upstream_ref.1) | copy-start | bytes 196612
  0.7 20.3 %copy-start.7 = (f32[256]{0:T(256)S(1)}, f32[256]{0:T(256)}, u32[]{:S(2)}) copy-start(f32[256]{0:T(256)} %param.22) | copy-start | bytes 3076
  0.7 20.3 %copy-start.1 = (bf16[128,256]{1,0:T(8,128)(2,1)S(1)}, bf16[128,256]{1,0:T(8,128)(2,1)}, u32[]{:S(2)}) copy-start(bf16[128,256]{1,0:T(8,128)(2,1)} %w_neigh_ref.1) | copy-start | bytes 196612
  0.7 20.3 %copy-start = (bf16[128,256]{1,0:T(8,128)(2,1)S(1)}, bf16[128,256]{1,0:T(8,128)(2,1)}, u32[]{:S(2)}) copy-start(bf16[128,256]{1,0:T(8,128)(2,1)} %w_self_ref.1) | copy-start | bytes 196612
  0.7 20.3 %copy-start.8 = (s32[128]{0:T(128)S(1)}, s32[128]{0:T(128)}, u32[]{:S(2)}) copy-start(s32[128]{0:T(128)} %param.19) | copy-start | bytes 1540
  0.7 20.3 %copy-start.3 = (bf16[128,128]{1,0:T(8,128)(2,1)S(1)}, bf16[128,128]{1,0:T(8,128)(2,1)}, u32[]{:S(2)}) copy-start(bf16[128,128]{1,0:T(8,128)(2,1)} %self_ref.1) | copy-start | bytes 98308

commit v8 on v7

--- a/solution.py
+++ b/solution.py
@@ -17,7 +17,7 @@
         return carry
 
     nfeat = order_ref.shape[0] // ncol
-    lax.fori_loop(0, nfeat, body, 0, unroll=max(1, 32 // ncol))
+    lax.fori_loop(0, nfeat, body, 0, unroll=max(1, 8 // ncol))
 
 
 def fetch(pairs, sems):

time: 34.7 us -> 34.3 us (0.988)
  Pallas kernels: 7.76 us -> 7.36 us
    pallas_call x1, Pallas kernels: 3.15 us -> 2.74 us  [local(): pl.pallas_call(functools.partial(backward_kernel, ncol), out_shape=(jax.S...]
where the time goes in v8:
time: 34.3 us; the launch traced here: 34 us
  blocking collectives  25.2 us (73%)
  Pallas kernels  7.36 us (21%)
  between operations  1.49 us (4%)
    all_to_all x1, blocking collectives, local(): lax.all_to_all(partial_value, ('col', 'feat'), split_axis=0, concat_axis=...  15.3 us
    all_to_all x1, blocking collectives, local(): lax.all_to_all(back.reshape(blocks_total, slice_width, tile_size), ('col'...  9.88 us
    pallas_call x1, Pallas kernels, local(): pl.pallas_call(forward_kernel, out_shape=(jax.ShapeDtypeStruct((blocks_to...  4.19 us
    pallas_call x1, Pallas kernels, local(): pl.pallas_call(functools.partial(backward_kernel, ncol), out_shape=(jax.S...  2.74 us

profile of v8, /device:TPU:0, one launch (start us, length us, event | category | flops | bytes accessed | tf_op | source)
XLA Modules:
  0.0 34.0 jit_solution(1515005986518365133)
XLA Ops:
  0.6 0.0 copy-start.6
  0.6 0.0 copy-start.5
  0.7 0.0 copy-start.4
  0.7 0.0 copy-start.2
  0.7 0.0 copy-start.7
  0.7 0.0 copy-start.1
  0.7 0.0 copy-start
  0.7 0.0 copy-start.8
  0.7 0.0 copy-start.3
  1.5 4.2 %forward.1 = (bf16[32,16,128]{2,1,0:T(8,128)(2,1)S(1)}, bf16[256,128,128]{2,1,0:T(8,128)(2,1)S(1)}) custom-call(s32[32]{0:T(128)} %order_ref.1, s32[256]{0:T(256)} %rows_ref.1, s32[256]{0:T(256)} %cols_ref.1, s32[1]{0:T(128)S(6)} %copy.14.count_hbm.count_ref, bf16[16,4096]{1,0:T(8,128)(2,1)} %feats_hbm.1, bf16[256,128,128]{2,1,0:T(8,128)(2,1)} %tiles_hbm.1), custom_call_target="tpu_custom_call" | custom-call | tf_op jit(solution)/shard_map/forward/pallas_call | solution.py:232
  5.7 15.3 %all_to_all.10 = bf16[32,16,128]{2,1,0:T(8,128)(2,1)S(1)} all-to-all(bf16[32,16,128]{2,1,0:T(8,128)(2,1)S(1)} %get-tuple-element.8), channel_id=1, replica_groups=mesh['feat'=8,'col'=4] {'col','feat'}, dimensions={0} | all-to-all | bytes 262144 | tf_op jit(solution)/shard_map/all_to_all | solution.py:253
  20.9 0.0 copy-done.2
  20.9 0.0 copy-done.7
  20.9 0.0 copy-done.1
  20.9 0.0 copy-done
  21.0 0.0 copy-done.8
  21.0 0.0 copy-done.3
  21.0 0.4 %dense.1 = (bf16[128,256]{1,0:T(8,128)(2,1)S(1)}, bf16[4,8,16,128]{3,2,1,0:T(8,128)(2,1)S(1)}) custom-call(bf16[4,8,16,128]{3,2,1,0:T(8,128)(2,1)S(1)} %bitcast.4, bf16[128,128]{1,0:T(8,128)(2,1)S(1)} %copy-done.3, s32[1,128]{1,0:T(1,128)S(1)} %bitcast.7, bf16[128,256]{1,0:T(8,128)(2,1)S(1)} %copy-done, bf16[128,256]{1,0:T(8,128)(2,1)S(1)} %copy-done.1, ...), custom_call_target="tpu_custom_call" | custom-call | tf_op jit(solution)/shard_map/dense/pallas_call | solution.py:255
  21.4 9.9 %all_to_all.11.grads_ref = bf16[32,16,128]{2,1,0:T(8,128)(2,1)S(1)} all-to-all(bf16[32,16,128]{2,1,0:T(8,128)(2,1)S(1)} %bitcast.5), channel_id=1, replica_groups=mesh['feat'=8,'col'=4] {'col','feat'}, dimensions={0} | all-to-all | bytes 262144 | tf_op jit(solution)/shard_map/all_to_all | solution.py:276
  31.3 0.0 copy-done.6
  31.3 0.0 copy-done.5
  31.3 0.0 copy-done.4
  31.3 2.7 %backward.1 = (bf16[16,4096]{1,0:T(8,128)(2,1)}, bf16[128,256]{1,0:T(8,128)(2,1)}) custom-call(s32[32]{0:T(128)S(1)} %copy-done.6, s32[256]{0:T(256)S(1)} %copy-done.4, s32[256]{0:T(256)S(1)} %copy-done.5, s32[1]{0:T(128)S(6)} %copy.14.count_hbm.count_ref, bf16[32,16,128]{2,1,0:T(8,128)(2,1)S(1)} %all_to_all.11.grads_ref, ...), custom_call_target="tpu_custom_call" | custom-call | tf_op jit(solution)/shard_map/backward/pallas_call | solution.py:284
Async XLA Ops:
  0.6 30.7 %copy-start.6 = (s32[32]{0:T(128)S(1)}, s32[32]{0:T(128)}, u32[]{:S(2)}) copy-start(s32[32]{0:T(128)} %order_ref.1) | copy-start | bytes 388
  0.6 30.7 %copy-start.5 = (s32[256]{0:T(256)S(1)}, s32[256]{0:T(256)}, u32[]{:S(2)}) copy-start(s32[256]{0:T(256)} %cols_ref.1) | copy-start | bytes 3076
  0.7 30.6 %copy-start.4 = (s32[256]{0:T(256)S(1)}, s32[256]{0:T(256)}, u32[]{:S(2)}) copy-start(s32[256]{0:T(256)} %rows_ref.1) | copy-start | bytes 3076
  0.7 20.3 %copy-start.2 = (bf16[128,256]{1,0:T(8,128)(2,1)S(1)}, bf16[128,256]{1,0:T(8,128)(2,1)}, u32[]{:S(2)}) copy-start(bf16[128,256]{1,0:T(8,128)(2,1)} %upstream_ref.1) | copy-start | bytes 196612
  0.7 20.3 %copy-start.7 = (f32[256]{0:T(256)S(1)}, f32[256]{0:T(256)}, u32[]{:S(2)}) copy-start(f32[256]{0:T(256)} %param.22) | copy-start | bytes 3076
  0.7 20.3 %copy-start.1 = (bf16[128,256]{1,0:T(8,128)(2,1)S(1)}, bf16[128,256]{1,0:T(8,128)(2,1)}, u32[]{:S(2)}) copy-start(bf16[128,256]{1,0:T(8,128)(2,1)} %w_neigh_ref.1) | copy-start | bytes 196612
  0.7 20.3 %copy-start = (bf16[128,256]{1,0:T(8,128)(2,1)S(1)}, bf16[128,256]{1,0:T(8,128)(2,1)}, u32[]{:S(2)}) copy-start(bf16[128,256]{1,0:T(8,128)(2,1)} %w_self_ref.1) | copy-start | bytes 196612
  0.7 20.3 %copy-start.8 = (s32[128]{0:T(128)S(1)}, s32[128]{0:T(128)}, u32[]{:S(2)}) copy-start(s32[128]{0:T(128)} %param.19) | copy-start | bytes 1540
  0.7 20.3 %copy-start.3 = (bf16[128,128]{1,0:T(8,128)(2,1)S(1)}, bf16[128,128]{1,0:T(8,128)(2,1)}, u32[]{:S(2)}) copy-start(bf16[128,128]{1,0:T(8,128)(2,1)} %self_ref.1) | copy-start | bytes 98308

commit v9 on v8

--- a/solution.py
+++ b/solution.py
@@ -50,13 +50,14 @@
     feats_hbm,
     tiles_hbm,
     partial_ref,
-    tiles_ref,
+    kept_ref,
     order_ref,
     rows_ref,
     cols_ref,
     count_ref,
     feats_ref,
     feat_blocks,
+    tiles_ref,
     places,
     small_sems,
     sems,
@@ -92,6 +93,7 @@
         if first % CHUNK == 0:
             tile_copy(tiles_hbm, tiles_ref, sems, first // CHUNK).wait()
         pair = (first, first + 1)
+        kept_ref[pl.ds(first, 2)] = tiles_ref[pl.ds(first, 2)].astype(kept_ref.dtype)
         feats = [feat_blocks[cols_ref[slot]] for slot in pair]
         packed = (tiles_ref[first] + two * tiles_ref[first + 1]).T
         odd = jnp.where(packed >= two, one, zero)
@@ -179,9 +181,10 @@
     for first in range(0, slots, 2):
         even = grads_ref[places[rows_ref[first]]]
         odd = grads_ref[places[rows_ref[first + 1]]]
-        pieces = jnp.dot(
+        pieces = lax.dot_general(
             block_diagonal(even, odd),
             tiles_ref[pl.ds(first, 2)].reshape(2 * tile_size, tile_size),
+            (((1,), (0,)), ((), ())),
             preferred_element_type=jnp.float32,
         )
         for i, acc in enumerate(accs):
@@ -233,7 +236,7 @@
         forward_kernel,
         out_shape=(
             jax.ShapeDtypeStruct((blocks_total, slice_width, tile_size), jnp.bfloat16),
-            pltpu.VMEM(tiles.shape, tiles.dtype),
+            pltpu.VMEM(tiles.shape, jnp.float8_e4m3fn),
         ),
         in_specs=[ANY] * 6,
         out_specs=(VMEM, VMEM),
@@ -241,6 +244,7 @@
         + [
             pltpu.VMEM(neighbour_feats.shape, neighbour_feats.dtype),
             pltpu.VMEM((col_blocks, slice_width, tile_size), neighbour_feats.dtype),
+            pltpu.VMEM(tiles.shape, tiles.dtype),
             pltpu.SMEM((blocks_total,), jnp.int32),
             pltpu.SemaphoreType.DMA((5,)),
             pltpu.SemaphoreType.DMA((slots // CHUNK,)),

time: 34.3 us -> 34 us (level)
    pallas_call x1, Pallas kernels: 2.74 us -> 2.26 us  [local(): pl.pallas_call(functools.partial(backward_kernel, ncol), out_shape=(jax.S...]
where the time goes in v9:
time: 34 us; the launch traced here: 33.7 us
  blocking collectives  25.2 us (74%)
  Pallas kernels  7.06 us (21%)
  between operations  1.49 us (4%)
    all_to_all x1, blocking collectives, local(): lax.all_to_all(partial_value, ('col', 'feat'), split_axis=0, concat_axis=...  15.3 us
    all_to_all x1, blocking collectives, local(): lax.all_to_all(back.reshape(blocks_total, slice_width, tile_size), ('col'...  9.88 us
    pallas_call x1, Pallas kernels, local(): pl.pallas_call(forward_kernel, out_shape=(jax.ShapeDtypeStruct((blocks_to...  4.37 us
    pallas_call x1, Pallas kernels, local(): pl.pallas_call(functools.partial(backward_kernel, ncol), out_shape=(jax.S...  2.26 us

profile of v9, /device:TPU:0, one launch (start us, length us, event | category | flops | bytes accessed | tf_op | source)
XLA Modules:
  0.0 33.7 jit_solution(2163404531256402327)
XLA Ops:
  0.6 0.0 copy-start.6
  0.6 0.0 copy-start.5
  0.7 0.0 copy-start.4
  0.7 0.0 copy-start.2
  0.7 0.0 copy-start.7
  0.7 0.0 copy-start.1
  0.7 0.0 copy-start
  0.7 0.0 copy-start.8
  0.7 0.0 copy-start.3
  1.5 4.4 %forward.1 = (bf16[32,16,128]{2,1,0:T(8,128)(2,1)S(1)}, f8e4m3fn[256,128,128]{2,1,0:T(32,128)(4,1)S(1)}) custom-call(s32[32]{0:T(128)} %order_ref.1, s32[256]{0:T(256)} %rows_ref.1, s32[256]{0:T(256)} %cols_ref.1, s32[1]{0:T(128)S(6)} %copy.14.count_hbm.count_ref, bf16[16,4096]{1,0:T(8,128)(2,1)} %feats_hbm.1, bf16[256,128,128]{2,1,0:T(8,128)(2,1)} %tiles_hbm.1), custom_call_target="tpu_custom_call" | custom-call | tf_op jit(solution)/shard_map/forward/pallas_call | solution.py:235
  5.8 15.3 %all_to_all.10 = bf16[32,16,128]{2,1,0:T(8,128)(2,1)S(1)} all-to-all(bf16[32,16,128]{2,1,0:T(8,128)(2,1)S(1)} %get-tuple-element.8), channel_id=1, replica_groups=mesh['feat'=8,'col'=4] {'col','feat'}, dimensions={0} | all-to-all | bytes 262144 | tf_op jit(solution)/shard_map/all_to_all | solution.py:257
  21.1 0.0 copy-done.2
  21.1 0.0 copy-done.7
  21.1 0.0 copy-done.1
  21.1 0.0 copy-done
  21.1 0.0 copy-done.8
  21.1 0.0 copy-done.3
  21.2 0.4 %dense.1 = (bf16[128,256]{1,0:T(8,128)(2,1)S(1)}, bf16[4,8,16,128]{3,2,1,0:T(8,128)(2,1)S(1)}) custom-call(bf16[4,8,16,128]{3,2,1,0:T(8,128)(2,1)S(1)} %bitcast.4, bf16[128,128]{1,0:T(8,128)(2,1)S(1)} %copy-done.3, s32[1,128]{1,0:T(1,128)S(1)} %bitcast.7, bf16[128,256]{1,0:T(8,128)(2,1)S(1)} %copy-done, bf16[128,256]{1,0:T(8,128)(2,1)S(1)} %copy-done.1, ...), custom_call_target="tpu_custom_call" | custom-call | tf_op jit(solution)/shard_map/dense/pallas_call | solution.py:259
  21.6 9.9 %all_to_all.11.grads_ref = bf16[32,16,128]{2,1,0:T(8,128)(2,1)S(1)} all-to-all(bf16[32,16,128]{2,1,0:T(8,128)(2,1)S(1)} %bitcast.5), channel_id=1, replica_groups=mesh['feat'=8,'col'=4] {'col','feat'}, dimensions={0} | all-to-all | bytes 262144 | tf_op jit(solution)/shard_map/all_to_all | solution.py:280
  31.5 0.0 copy-done.6
  31.5 0.0 copy-done.5
  31.5 0.0 copy-done.4
  31.5 2.3 %backward.1 = (bf16[16,4096]{1,0:T(8,128)(2,1)}, bf16[128,256]{1,0:T(8,128)(2,1)}) custom-call(s32[32]{0:T(128)S(1)} %copy-done.6, s32[256]{0:T(256)S(1)} %copy-done.4, s32[256]{0:T(256)S(1)} %copy-done.5, s32[1]{0:T(128)S(6)} %copy.14.count_hbm.count_ref, bf16[32,16,128]{2,1,0:T(8,128)(2,1)S(1)} %all_to_all.11.grads_ref, ...), custom_call_target="tpu_custom_call" | custom-call | tf_op jit(solution)/shard_map/backward/pallas_call | solution.py:288
Async XLA Ops:
  0.6 30.8 %copy-start.6 = (s32[32]{0:T(128)S(1)}, s32[32]{0:T(128)}, u32[]{:S(2)}) copy-start(s32[32]{0:T(128)} %order_ref.1) | copy-start | bytes 388
  0.6 30.8 %copy-start.5 = (s32[256]{0:T(256)S(1)}, s32[256]{0:T(256)}, u32[]{:S(2)}) copy-start(s32[256]{0:T(256)} %cols_ref.1) | copy-start | bytes 3076
  0.7 30.8 %copy-start.4 = (s32[256]{0:T(256)S(1)}, s32[256]{0:T(256)}, u32[]{:S(2)}) copy-start(s32[256]{0:T(256)} %rows_ref.1) | copy-start | bytes 3076
  0.7 20.5 %copy-start.2 = (bf16[128,256]{1,0:T(8,128)(2,1)S(1)}, bf16[128,256]{1,0:T(8,128)(2,1)}, u32[]{:S(2)}) copy-start(bf16[128,256]{1,0:T(8,128)(2,1)} %upstream_ref.1) | copy-start | bytes 196612
  0.7 20.4 %copy-start.7 = (f32[256]{0:T(256)S(1)}, f32[256]{0:T(256)}, u32[]{:S(2)}) copy-start(f32[256]{0:T(256)} %param.22) | copy-start | bytes 3076
  0.7 20.4 %copy-start.1 = (bf16[128,256]{1,0:T(8,128)(2,1)S(1)}, bf16[128,256]{1,0:T(8,128)(2,1)}, u32[]{:S(2)}) copy-start(bf16[128,256]{1,0:T(8,128)(2,1)} %w_neigh_ref.1) | copy-start | bytes 196612
  0.7 20.4 %copy-start = (bf16[128,256]{1,0:T(8,128)(2,1)S(1)}, bf16[128,256]{1,0:T(8,128)(2,1)}, u32[]{:S(2)}) copy-start(bf16[128,256]{1,0:T(8,128)(2,1)} %w_self_ref.1) | copy-start | bytes 196612
  0.7 20.4 %copy-start.8 = (s32[128]{0:T(128)S(1)}, s32[128]{0:T(128)}, u32[]{:S(2)}) copy-start(s32[128]{0:T(128)} %param.19) | copy-start | bytes 1540
  0.7 20.4 %copy-start.3 = (bf16[128,128]{1,0:T(8,128)(2,1)S(1)}, bf16[128,128]{1,0:T(8,128)(2,1)}, u32[]{:S(2)}) copy-start(bf16[128,128]{1,0:T(8,128)(2,1)} %self_ref.1) | copy-start | bytes 98308

commit v10 on v9

--- a/solution.py
+++ b/solution.py
@@ -87,20 +87,19 @@
         feat_blocks[block] = feats_ref[:, block * tile_size : (block + 1) * tile_size]
     invert_order(order_ref, places, ncol, lambda feat, col: feat)
     count = count_ref[0]
-    zero, one, two = (jnp.asarray(v, tiles_ref.dtype) for v in (0, 1, 2))
 
     for first in range(0, slots, 2):
         if first % CHUNK == 0:
             tile_copy(tiles_hbm, tiles_ref, sems, first // CHUNK).wait()
         pair = (first, first + 1)
-        kept_ref[pl.ds(first, 2)] = tiles_ref[pl.ds(first, 2)].astype(kept_ref.dtype)
+        kept = [tiles_ref[slot].astype(kept_ref.dtype) for slot in pair]
+        for slot, tile in zip(pair, kept):
+            kept_ref[slot] = tile
         feats = [feat_blocks[cols_ref[slot]] for slot in pair]
-        packed = (tiles_ref[first] + two * tiles_ref[first + 1]).T
-        odd = jnp.where(packed >= two, one, zero)
-        even = packed - two * odd
-        pieces = jnp.dot(
+        pieces = lax.dot_general(
             block_diagonal(*feats),
-            jnp.concatenate([even, odd], axis=0),
+            jnp.concatenate([tile.T for tile in kept], axis=0),
+            (((1,), (0,)), ((), ())),
             preferred_element_type=jnp.float32,
         )
         for i, slot in enumerate(pair):

time: 34 us -> 33.7 us (level)
  no operation moved by 1% of the time
where the time goes in v10:
time: 33.7 us; the launch traced here: 33.6 us
  blocking collectives  25.1 us (74%)
  Pallas kernels  6.88 us (20%)
  between operations  1.5 us (4%)
    all_to_all x1, blocking collectives, local(): lax.all_to_all(partial_value, ('col', 'feat'), split_axis=0, concat_axis=...  15.3 us
    all_to_all x1, blocking collectives, local(): lax.all_to_all(back.reshape(blocks_total, slice_width, tile_size), ('col'...  9.88 us
    pallas_call x1, Pallas kernels, local(): pl.pallas_call(forward_kernel, out_shape=(jax.ShapeDtypeStruct((blocks_to...  4.12 us
    pallas_call x1, Pallas kernels, local(): pl.pallas_call(functools.partial(backward_kernel, ncol), out_shape=(jax.S...  2.33 us

profile of v10, /device:TPU:0, one launch (start us, length us, event | category | flops | bytes accessed | tf_op | source)
XLA Modules:
  0.0 33.6 jit_solution(4021804514897278452)
XLA Ops:
  0.6 0.0 copy-start.6
  0.6 0.0 copy-start.5
  0.7 0.0 copy-start.4
  0.7 0.0 copy-start.2
  0.7 0.0 copy-start.7
  0.7 0.0 copy-start.1
  0.7 0.0 copy-start
  0.7 0.0 copy-start.8
  0.7 0.0 copy-start.3
  1.5 4.1 %forward.1 = (bf16[32,16,128]{2,1,0:T(8,128)(2,1)S(1)}, f8e4m3fn[256,128,128]{2,1,0:T(32,128)(4,1)S(1)}) custom-call(s32[32]{0:T(128)} %order_ref.1, s32[256]{0:T(256)} %rows_ref.1, s32[256]{0:T(256)} %cols_ref.1, s32[1]{0:T(128)S(6)} %copy.14.count_hbm.count_ref, bf16[16,4096]{1,0:T(8,128)(2,1)} %feats_hbm.1, bf16[256,128,128]{2,1,0:T(8,128)(2,1)} %tiles_hbm.1), custom_call_target="tpu_custom_call" | custom-call | tf_op jit(solution)/shard_map/forward/pallas_call | solution.py:234
  5.6 15.3 %all_to_all.10 = bf16[32,16,128]{2,1,0:T(8,128)(2,1)S(1)} all-to-all(bf16[32,16,128]{2,1,0:T(8,128)(2,1)S(1)} %get-tuple-element.8), channel_id=1, replica_groups=mesh['feat'=8,'col'=4] {'col','feat'}, dimensions={0} | all-to-all | bytes 262144 | tf_op jit(solution)/shard_map/all_to_all | solution.py:256
  20.9 0.0 copy-done.2
  20.9 0.0 copy-done.7
  20.9 0.0 copy-done.1
  20.9 0.0 copy-done
  20.9 0.0 copy-done.8
  20.9 0.0 copy-done.3
  20.9 0.4 %dense.1 = (bf16[128,256]{1,0:T(8,128)(2,1)S(1)}, bf16[4,8,16,128]{3,2,1,0:T(8,128)(2,1)S(1)}) custom-call(bf16[4,8,16,128]{3,2,1,0:T(8,128)(2,1)S(1)} %bitcast.4, bf16[128,128]{1,0:T(8,128)(2,1)S(1)} %copy-done.3, s32[1,128]{1,0:T(1,128)S(1)} %bitcast.7, bf16[128,256]{1,0:T(8,128)(2,1)S(1)} %copy-done, bf16[128,256]{1,0:T(8,128)(2,1)S(1)} %copy-done.1, ...), custom_call_target="tpu_custom_call" | custom-call | tf_op jit(solution)/shard_map/dense/pallas_call | solution.py:258
  21.3 9.9 %all_to_all.11.grads_ref = bf16[32,16,128]{2,1,0:T(8,128)(2,1)S(1)} all-to-all(bf16[32,16,128]{2,1,0:T(8,128)(2,1)S(1)} %bitcast.5), channel_id=1, replica_groups=mesh['feat'=8,'col'=4] {'col','feat'}, dimensions={0} | all-to-all | bytes 262144 | tf_op jit(solution)/shard_map/all_to_all | solution.py:279
  31.2 0.0 copy-done.6
  31.2 0.0 copy-done.5
  31.2 0.0 copy-done.4
  31.2 2.3 %backward.1 = (bf16[16,4096]{1,0:T(8,128)(2,1)}, bf16[128,256]{1,0:T(8,128)(2,1)}) custom-call(s32[32]{0:T(128)S(1)} %copy-done.6, s32[256]{0:T(256)S(1)} %copy-done.4, s32[256]{0:T(256)S(1)} %copy-done.5, s32[1]{0:T(128)S(6)} %copy.14.count_hbm.count_ref, bf16[32,16,128]{2,1,0:T(8,128)(2,1)S(1)} %all_to_all.11.grads_ref, ...), custom_call_target="tpu_custom_call" | custom-call | tf_op jit(solution)/shard_map/backward/pallas_call | solution.py:287
Async XLA Ops:
  0.6 30.6 %copy-start.6 = (s32[32]{0:T(128)S(1)}, s32[32]{0:T(128)}, u32[]{:S(2)}) copy-start(s32[32]{0:T(128)} %order_ref.1) | copy-start | bytes 388
  0.6 30.6 %copy-start.5 = (s32[256]{0:T(256)S(1)}, s32[256]{0:T(256)}, u32[]{:S(2)}) copy-start(s32[256]{0:T(256)} %cols_ref.1) | copy-start | bytes 3076
  0.7 30.6 %copy-start.4 = (s32[256]{0:T(256)S(1)}, s32[256]{0:T(256)}, u32[]{:S(2)}) copy-start(s32[256]{0:T(256)} %rows_ref.1) | copy-start | bytes 3076
  0.7 20.2 %copy-start.2 = (bf16[128,256]{1,0:T(8,128)(2,1)S(1)}, bf16[128,256]{1,0:T(8,128)(2,1)}, u32[]{:S(2)}) copy-start(bf16[128,256]{1,0:T(8,128)(2,1)} %upstream_ref.1) | copy-start | bytes 196612
  0.7 20.2 %copy-start.7 = (f32[256]{0:T(256)S(1)}, f32[256]{0:T(256)}, u32[]{:S(2)}) copy-start(f32[256]{0:T(256)} %param.22) | copy-start | bytes 3076
  0.7 20.2 %copy-start.1 = (bf16[128,256]{1,0:T(8,128)(2,1)S(1)}, bf16[128,256]{1,0:T(8,128)(2,1)}, u32[]{:S(2)}) copy-start(bf16[128,256]{1,0:T(8,128)(2,1)} %w_neigh_ref.1) | copy-start | bytes 196612
  0.7 20.2 %copy-start = (bf16[128,256]{1,0:T(8,128)(2,1)S(1)}, bf16[128,256]{1,0:T(8,128)(2,1)}, u32[]{:S(2)}) copy-start(bf16[128,256]{1,0:T(8,128)(2,1)} %w_self_ref.1) | copy-start | bytes 196612
  0.7 20.2 %copy-start.8 = (s32[128]{0:T(128)S(1)}, s32[128]{0:T(128)}, u32[]{:S(2)}) copy-start(s32[128]{0:T(128)} %param.19) | copy-start | bytes 1540
  0.7 20.2 %copy-start.3 = (bf16[128,128]{1,0:T(8,128)(2,1)S(1)}, bf16[128,128]{1,0:T(8,128)(2,1)}, u32[]{:S(2)}) copy-start(bf16[128,128]{1,0:T(8,128)(2,1)} %self_ref.1) | copy-start | bytes 98308

commit v11 on v10

--- a/solution.py
+++ b/solution.py
@@ -7,7 +7,7 @@
 from jax.experimental.pallas import tpu as pltpu
 from jax.sharding import PartitionSpec as P
 
-CHUNK = 64
+CHUNK = 32
 
 
 def invert_order(order_ref, places, ncol, value):

time: 33.7 us -> 33.7 us (level)
  no operation moved by 1% of the time
where the time goes in v11:
time: 33.7 us; the launch traced here: 33.4 us
  blocking collectives  25.2 us (75%)
  Pallas kernels  6.74 us (20%)
  between operations  1.49 us (4%)
    all_to_all x1, blocking collectives, local(): lax.all_to_all(partial_value, ('col', 'feat'), split_axis=0, concat_axis=...  15.3 us
    all_to_all x1, blocking collectives, local(): lax.all_to_all(back.reshape(blocks_total, slice_width, tile_size), ('col'...  9.88 us
    pallas_call x1, Pallas kernels, local(): pl.pallas_call(forward_kernel, out_shape=(jax.ShapeDtypeStruct((blocks_to...  4.08 us
    pallas_call x1, Pallas kernels, local(): pl.pallas_call(functools.partial(backward_kernel, ncol), out_shape=(jax.S...  2.24 us

profile of v11, /device:TPU:0, one launch (start us, length us, event | category | flops | bytes accessed | tf_op | source)
XLA Modules:
  0.0 33.4 jit_solution(8417361132697438989)
XLA Ops:
  0.6 0.0 copy-start.6
  0.6 0.0 copy-start.5
  0.7 0.0 copy-start.4
  0.7 0.0 copy-start.2
  0.7 0.0 copy-start.7
  0.7 0.0 copy-start.1
  0.7 0.0 copy-start
  0.7 0.0 copy-start.8
  0.7 0.0 copy-start.3
  1.5 4.1 %forward.1 = (bf16[32,16,128]{2,1,0:T(8,128)(2,1)S(1)}, f8e4m3fn[256,128,128]{2,1,0:T(32,128)(4,1)S(1)}) custom-call(s32[32]{0:T(128)} %order_ref.1, s32[256]{0:T(256)} %rows_ref.1, s32[256]{0:T(256)} %cols_ref.1, s32[1]{0:T(128)S(6)} %copy.14.count_hbm.count_ref, bf16[16,4096]{1,0:T(8,128)(2,1)} %feats_hbm.1, bf16[256,128,128]{2,1,0:T(8,128)(2,1)} %tiles_hbm.1), custom_call_target="tpu_custom_call" | custom-call | tf_op jit(solution)/shard_map/forward/pallas_call | solution.py:234
  5.5 15.3 %all_to_all.10 = bf16[32,16,128]{2,1,0:T(8,128)(2,1)S(1)} all-to-all(bf16[32,16,128]{2,1,0:T(8,128)(2,1)S(1)} %get-tuple-element.8), channel_id=1, replica_groups=mesh['feat'=8,'col'=4] {'col','feat'}, dimensions={0} | all-to-all | bytes 262144 | tf_op jit(solution)/shard_map/all_to_all | solution.py:256
  20.8 0.0 copy-done.2
  20.8 0.0 copy-done.7
  20.8 0.0 copy-done.1
  20.8 0.0 copy-done
  20.9 0.0 copy-done.8
  20.9 0.0 copy-done.3
  20.9 0.4 %dense.1 = (bf16[128,256]{1,0:T(8,128)(2,1)S(1)}, bf16[4,8,16,128]{3,2,1,0:T(8,128)(2,1)S(1)}) custom-call(bf16[4,8,16,128]{3,2,1,0:T(8,128)(2,1)S(1)} %bitcast.4, bf16[128,128]{1,0:T(8,128)(2,1)S(1)} %copy-done.3, s32[1,128]{1,0:T(1,128)S(1)} %bitcast.7, bf16[128,256]{1,0:T(8,128)(2,1)S(1)} %copy-done, bf16[128,256]{1,0:T(8,128)(2,1)S(1)} %copy-done.1, ...), custom_call_target="tpu_custom_call" | custom-call | tf_op jit(solution)/shard_map/dense/pallas_call | solution.py:258
  21.3 9.9 %all_to_all.11.grads_ref = bf16[32,16,128]{2,1,0:T(8,128)(2,1)S(1)} all-to-all(bf16[32,16,128]{2,1,0:T(8,128)(2,1)S(1)} %bitcast.5), channel_id=1, replica_groups=mesh['feat'=8,'col'=4] {'col','feat'}, dimensions={0} | all-to-all | bytes 262144 | tf_op jit(solution)/shard_map/all_to_all | solution.py:279
  31.2 0.0 copy-done.6
  31.2 0.0 copy-done.5
  31.2 0.0 copy-done.4
  31.2 2.2 %backward.1 = (bf16[16,4096]{1,0:T(8,128)(2,1)}, bf16[128,256]{1,0:T(8,128)(2,1)}) custom-call(s32[32]{0:T(128)S(1)} %copy-done.6, s32[256]{0:T(256)S(1)} %copy-done.4, s32[256]{0:T(256)S(1)} %copy-done.5, s32[1]{0:T(128)S(6)} %copy.14.count_hbm.count_ref, bf16[32,16,128]{2,1,0:T(8,128)(2,1)S(1)} %all_to_all.11.grads_ref, ...), custom_call_target="tpu_custom_call" | custom-call | tf_op jit(solution)/shard_map/backward/pallas_call | solution.py:287
Async XLA Ops:
  0.6 30.6 %copy-start.6 = (s32[32]{0:T(128)S(1)}, s32[32]{0:T(128)}, u32[]{:S(2)}) copy-start(s32[32]{0:T(128)} %order_ref.1) | copy-start | bytes 388
  0.6 30.6 %copy-start.5 = (s32[256]{0:T(256)S(1)}, s32[256]{0:T(256)}, u32[]{:S(2)}) copy-start(s32[256]{0:T(256)} %cols_ref.1) | copy-start | bytes 3076
  0.7 30.5 %copy-start.4 = (s32[256]{0:T(256)S(1)}, s32[256]{0:T(256)}, u32[]{:S(2)}) copy-start(s32[256]{0:T(256)} %rows_ref.1) | copy-start | bytes 3076
  0.7 20.2 %copy-start.2 = (bf16[128,256]{1,0:T(8,128)(2,1)S(1)}, bf16[128,256]{1,0:T(8,128)(2,1)}, u32[]{:S(2)}) copy-start(bf16[128,256]{1,0:T(8,128)(2,1)} %upstream_ref.1) | copy-start | bytes 196612
  0.7 20.2 %copy-start.7 = (f32[256]{0:T(256)S(1)}, f32[256]{0:T(256)}, u32[]{:S(2)}) copy-start(f32[256]{0:T(256)} %param.22) | copy-start | bytes 3076
  0.7 20.2 %copy-start.1 = (bf16[128,256]{1,0:T(8,128)(2,1)S(1)}, bf16[128,256]{1,0:T(8,128)(2,1)}, u32[]{:S(2)}) copy-start(bf16[128,256]{1,0:T(8,128)(2,1)} %w_neigh_ref.1) | copy-start | bytes 196612
  0.7 20.1 %copy-start = (bf16[128,256]{1,0:T(8,128)(2,1)S(1)}, bf16[128,256]{1,0:T(8,128)(2,1)}, u32[]{:S(2)}) copy-start(bf16[128,256]{1,0:T(8,128)(2,1)} %w_self_ref.1) | copy-start | bytes 196612
  0.7 20.1 %copy-start.8 = (s32[128]{0:T(128)S(1)}, s32[128]{0:T(128)}, u32[]{:S(2)}) copy-start(s32[128]{0:T(128)} %param.19) | copy-start | bytes 1540
  0.7 20.1 %copy-start.3 = (bf16[128,128]{1,0:T(8,128)(2,1)S(1)}, bf16[128,128]{1,0:T(8,128)(2,1)}, u32[]{:S(2)}) copy-start(bf16[128,128]{1,0:T(8,128)(2,1)} %self_ref.1) | copy-start | bytes 98308

commit v12 on v10

--- a/solution.py
+++ b/solution.py
@@ -67,6 +67,8 @@
     blocks_total, slice_width, _ = partial_ref.shape
     ncol = len(accs)
     nfeat = blocks_total // ncol
+    for chunk in range(slots // CHUNK):
+        tile_copy(tiles_hbm, tiles_ref, sems, chunk).start(priority=1)
     small = fetch(
         [
             (order_hbm, order_ref),
@@ -77,8 +79,6 @@
         ],
         small_sems,
     )
-    for chunk in range(slots // CHUNK):
-        tile_copy(tiles_hbm, tiles_ref, sems, chunk).start(priority=1)
     for acc in accs:
         acc[...] = jnp.zeros_like(acc)
     for copy in small:

time: 33.7 us -> 33.7 us (level)
  no operation moved by 1% of the time
where the time goes in v12:
time: 33.7 us; the launch traced here: 33.6 us
  blocking collectives  25.2 us (75%)
  Pallas kernels  6.88 us (20%)
  between operations  1.49 us (4%)
    all_to_all x1, blocking collectives, local(): lax.all_to_all(partial_value, ('col', 'feat'), split_axis=0, concat_axis=...  15.3 us
    all_to_all x1, blocking collectives, local(): lax.all_to_all(back.reshape(blocks_total, slice_width, tile_size), ('col'...  9.88 us
    pallas_call x1, Pallas kernels, local(): pl.pallas_call(forward_kernel, out_shape=(jax.ShapeDtypeStruct((blocks_to...  4.12 us
    pallas_call x1, Pallas kernels, local(): pl.pallas_call(functools.partial(backward_kernel, ncol), out_shape=(jax.S...  2.33 us

profile of v12, /device:TPU:0, one launch (start us, length us, event | category | flops | bytes accessed | tf_op | source)
XLA Modules:
  0.0 33.6 jit_solution(9952385048514113088)
XLA Ops:
  0.6 0.0 copy-start.6
  0.6 0.0 copy-start.5
  0.7 0.0 copy-start.4
  0.7 0.0 copy-start.2
  0.7 0.0 copy-start.7
  0.7 0.0 copy-start.1
  0.7 0.0 copy-start
  0.7 0.0 copy-start.8
  0.7 0.0 copy-start.3
  1.5 4.1 %forward.1 = (bf16[32,16,128]{2,1,0:T(8,128)(2,1)S(1)}, f8e4m3fn[256,128,128]{2,1,0:T(32,128)(4,1)S(1)}) custom-call(s32[32]{0:T(128)} %order_ref.1, s32[256]{0:T(256)} %rows_ref.1, s32[256]{0:T(256)} %cols_ref.1, s32[1]{0:T(128)S(6)} %copy.14.count_hbm.count_ref, bf16[16,4096]{1,0:T(8,128)(2,1)} %feats_hbm.1, bf16[256,128,128]{2,1,0:T(8,128)(2,1)} %tiles_hbm.1), custom_call_target="tpu_custom_call" | custom-call | tf_op jit(solution)/shard_map/forward/pallas_call | solution.py:234
  5.6 15.3 %all_to_all.10 = bf16[32,16,128]{2,1,0:T(8,128)(2,1)S(1)} all-to-all(bf16[32,16,128]{2,1,0:T(8,128)(2,1)S(1)} %get-tuple-element.8), channel_id=1, replica_groups=mesh['feat'=8,'col'=4] {'col','feat'}, dimensions={0} | all-to-all | bytes 262144 | tf_op jit(solution)/shard_map/all_to_all | solution.py:256
  20.9 0.0 copy-done.2
  20.9 0.0 copy-done.7
  20.9 0.0 copy-done.1
  20.9 0.0 copy-done
  20.9 0.0 copy-done.8
  20.9 0.0 copy-done.3
  20.9 0.4 %dense.1 = (bf16[128,256]{1,0:T(8,128)(2,1)S(1)}, bf16[4,8,16,128]{3,2,1,0:T(8,128)(2,1)S(1)}) custom-call(bf16[4,8,16,128]{3,2,1,0:T(8,128)(2,1)S(1)} %bitcast.4, bf16[128,128]{1,0:T(8,128)(2,1)S(1)} %copy-done.3, s32[1,128]{1,0:T(1,128)S(1)} %bitcast.7, bf16[128,256]{1,0:T(8,128)(2,1)S(1)} %copy-done, bf16[128,256]{1,0:T(8,128)(2,1)S(1)} %copy-done.1, ...), custom_call_target="tpu_custom_call" | custom-call | tf_op jit(solution)/shard_map/dense/pallas_call | solution.py:258
  21.3 9.9 %all_to_all.11.grads_ref = bf16[32,16,128]{2,1,0:T(8,128)(2,1)S(1)} all-to-all(bf16[32,16,128]{2,1,0:T(8,128)(2,1)S(1)} %bitcast.5), channel_id=1, replica_groups=mesh['feat'=8,'col'=4] {'col','feat'}, dimensions={0} | all-to-all | bytes 262144 | tf_op jit(solution)/shard_map/all_to_all | solution.py:279
  31.2 0.0 copy-done.6
  31.2 0.0 copy-done.5
  31.2 0.0 copy-done.4
  31.2 2.3 %backward.1 = (bf16[16,4096]{1,0:T(8,128)(2,1)}, bf16[128,256]{1,0:T(8,128)(2,1)}) custom-call(s32[32]{0:T(128)S(1)} %copy-done.6, s32[256]{0:T(256)S(1)} %copy-done.4, s32[256]{0:T(256)S(1)} %copy-done.5, s32[1]{0:T(128)S(6)} %copy.14.count_hbm.count_ref, bf16[32,16,128]{2,1,0:T(8,128)(2,1)S(1)} %all_to_all.11.grads_ref, ...), custom_call_target="tpu_custom_call" | custom-call | tf_op jit(solution)/shard_map/backward/pallas_call | solution.py:287
Async XLA Ops:
  0.6 30.6 %copy-start.6 = (s32[32]{0:T(128)S(1)}, s32[32]{0:T(128)}, u32[]{:S(2)}) copy-start(s32[32]{0:T(128)} %order_ref.1) | copy-start | bytes 388
  0.6 30.6 %copy-start.5 = (s32[256]{0:T(256)S(1)}, s32[256]{0:T(256)}, u32[]{:S(2)}) copy-start(s32[256]{0:T(256)} %cols_ref.1) | copy-start | bytes 3076
  0.7 30.6 %copy-start.4 = (s32[256]{0:T(256)S(1)}, s32[256]{0:T(256)}, u32[]{:S(2)}) copy-start(s32[256]{0:T(256)} %rows_ref.1) | copy-start | bytes 3076
  0.7 20.2 %copy-start.2 = (bf16[128,256]{1,0:T(8,128)(2,1)S(1)}, bf16[128,256]{1,0:T(8,128)(2,1)}, u32[]{:S(2)}) copy-start(bf16[128,256]{1,0:T(8,128)(2,1)} %upstream_ref.1) | copy-start | bytes 196612
  0.7 20.2 %copy-start.7 = (f32[256]{0:T(256)S(1)}, f32[256]{0:T(256)}, u32[]{:S(2)}) copy-start(f32[256]{0:T(256)} %param.22) | copy-start | bytes 3076
  0.7 20.2 %copy-start.1 = (bf16[128,256]{1,0:T(8,128)(2,1)S(1)}, bf16[128,256]{1,0:T(8,128)(2,1)}, u32[]{:S(2)}) copy-start(bf16[128,256]{1,0:T(8,128)(2,1)} %w_neigh_ref.1) | copy-start | bytes 196612
  0.7 20.2 %copy-start = (bf16[128,256]{1,0:T(8,128)(2,1)S(1)}, bf16[128,256]{1,0:T(8,128)(2,1)}, u32[]{:S(2)}) copy-start(bf16[128,256]{1,0:T(8,128)(2,1)} %w_self_ref.1) | copy-start | bytes 196612
  0.7 20.2 %copy-start.8 = (s32[128]{0:T(128)S(1)}, s32[128]{0:T(128)}, u32[]{:S(2)}) copy-start(s32[128]{0:T(128)} %param.19) | copy-start | bytes 1540
  0.7 20.2 %copy-start.3 = (bf16[128,128]{1,0:T(8,128)(2,1)S(1)}, bf16[128,128]{1,0:T(8,128)(2,1)}, u32[]{:S(2)}) copy-start(bf16[128,128]{1,0:T(8,128)(2,1)} %self_ref.1) | copy-start | bytes 98308
